TPU v7x, 32 devices: a whole 2x2x4 slice. The times are simulated.
32 devices in a mesh: grp: 4 (over z), gz: 8 (over y, x, core).
Axes of the slice: x: 2, y: 2, z: 4, core: 2. Of those that a mesh axis runs over, the one named last changes fastest.
Arguments:
- load: float32 [3, 256, 64, 128], P(None, ('grp', 'gz')), may hold values from -128 to 128
- phases: int32 [256, 64, 128], P(('grp', 'gz')), may hold values from 0 to 3
- clamp: int32 [64, 128], replicated, may hold values 0 or 1
- phase_moduli: float32 [4], replicated, may hold values from 0.05 to 1
Outputs:
- displacement: float32 [3, 256, 64, 128], P(None, ('grp', 'gz'))
- residual: float32 [3, 256, 64, 128], P(None, ('grp', 'gz'))
All inputs are finite; a program needn't handle non-finite values.
Results may differ from a plain program's by a relative error of at most 0.0003.
Values sent between devices are 32-bit elements; how exact they have to be, the bound alone decides.
A program may use at most 128 MiB of HBM per device.

v0:
```python
import math

import jax
import jax.numpy as jnp
import numpy as np
from jax import lax
from jax.sharding import PartitionSpec as P

PHASES = 4
COARSEN = 8
CHEB = 4
ITERS = 2


CORNER_OFFSETS = [
    (along_z, along_y, along_x) for along_z in (0, 1) for along_y in (0, 1) for along_x in (0, 1)
]


def passed_along(value, axis, by):
    size = lax.axis_size(axis)
    pairs = [(i, i + by) for i in range(size) if 0 <= i + by < size]
    return lax.ppermute(value, axis, pairs)


def spread(block, axis, holder):
    block = jnp.where(lax.axis_index(axis) == holder, block, jnp.zeros_like(block))
    return lax.psum(block, axis)


def element_matrix():
    poisson = 0.3
    lame_first = poisson / ((1.0 + poisson) * (1.0 - 2.0 * poisson))
    shear = 1.0 / (2.0 * (1.0 + poisson))
    elastic = np.zeros((6, 6))
    elastic[:3, :3] = lame_first
    for axis_one in range(3):
        elastic[axis_one, axis_one] = lame_first + 2.0 * shear
        elastic[axis_one + 3, axis_one + 3] = shear
    points = [0.5 - 0.5 / math.sqrt(3.0), 0.5 + 0.5 / math.sqrt(3.0)]
    pairs = [(0, 1), (1, 2), (0, 2)]
    matrix = np.zeros((24, 24))
    for first_point in points:
        for second_point in points:
            for third_point in points:
                spot = (first_point, second_point, third_point)
                strain = np.zeros((6, 24))
                for corner, offset in enumerate(CORNER_OFFSETS):
                    values = [
                        spot[axis_one] if offset[axis_one] else 1.0 - spot[axis_one]
                        for axis_one in range(3)
                    ]
                    slopes = [1.0 if offset[axis_one] else -1.0 for axis_one in range(3)]
                    slants = []
                    for axis_one in range(3):
                        others = [values[axis_two] for axis_two in range(3) if axis_two != axis_one]
                        slants.append(slopes[axis_one] * others[0] * others[1])
                        strain[axis_one, 3 * corner + axis_one] = slants[axis_one]
                    for position, pair in enumerate(pairs):
                        strain[3 + position, 3 * corner + pair[0]] = slants[pair[1]]
                        strain[3 + position, 3 * corner + pair[1]] = slants[pair[0]]
                matrix = matrix + 0.125 * (strain.T @ elastic @ strain)
    return matrix


def spectral_bound(numbers):
    diagonal_part = np.array([numbers[index, index] for index in range(numbers.shape[0])])
    return float(np.max(np.sum(np.abs(numbers), axis=1) / diagonal_part))


def element_forces(extended, moduli, matrix):
    layers = moduli.shape[0]
    width = min(4, layers)
    blocks = (layers + width - 1) // width
    plane = tuple(extended.shape[2:])

    def add_block(total, index):
        start = index * width
        nodes = lax.dynamic_slice_in_dim(extended, start, width + 1, 1)
        weights = lax.dynamic_slice_in_dim(moduli, start, width, 0)
        gathered = jnp.stack(
            [
                jnp.roll(nodes[:, along_z : along_z + width], (-along_y, -along_x), (2, 3))
                for along_z, along_y, along_x in CORNER_OFFSETS
            ],
            0,
        )
        gathered = gathered.reshape((24, width) + plane)
        forces = (
            jnp.einsum("ij,jzyx->izyx", matrix, gathered, precision=lax.Precision.HIGHEST) * weights
        )
        forces = forces.reshape((8, 3, width) + plane)
        update = jnp.zeros((3, width + 1) + plane, jnp.float32)
        for corner, offset in enumerate(CORNER_OFFSETS):
            update = update.at[:, offset[0] : offset[0] + width].add(
                jnp.roll(forces[corner], (offset[1], offset[2]), (2, 3))
            )
        current = lax.dynamic_slice_in_dim(total, start, width + 1, 1)
        return (lax.dynamic_update_slice_in_dim(total, current + update, start, 1), None)

    initial = jnp.zeros(extended.shape, jnp.float32)
    total, unused = lax.scan(add_block, initial, jnp.arange(blocks, dtype=jnp.int32))
    return total[:, : layers + 1]


def node_diagonal(lower, moduli, matrix):
    layers = moduli.shape[0]
    extended = jnp.concatenate([lower, moduli], 0)
    entries = jnp.diagonal(matrix).reshape(8, 3)
    total = jnp.zeros((3,) + tuple(moduli.shape), jnp.float32)
    for corner, offset in enumerate(CORNER_OFFSETS):
        shifted = jnp.roll(
            extended[1 - offset[0] : 1 - offset[0] + layers], (offset[1], offset[2]), (1, 2)
        )
        total = total + entries[corner][:, None, None, None] * shifted[None]
    return total


def chebyshev(rhs, coarse_apply, coarse_inverse, bound, sweeps):
    bottom = bound / 20.0
    center = 0.5 * (bound + bottom)
    radius = 0.5 * (bound - bottom)
    sigma = center / radius
    rho = 1.0 / sigma
    update = coarse_inverse * rhs / center
    correction = update
    remainder = rhs
    for sweep in range(sweeps - 1):
        remainder = remainder - coarse_apply(update)
        rho_next = 1.0 / (2.0 * sigma - rho)
        update = rho_next * rho * update + 2.0 * rho_next / radius * coarse_inverse * remainder
        correction = correction + update
        rho = rho_next
    return correction


def restrict(field, factor):
    comps, layers, height, breadth = field.shape
    return field.reshape(
        comps, layers // factor, factor, height // factor, factor, breadth // factor, factor
    ).sum((2, 4, 6))


def prolong(coarse, factor):
    comps, layers, height, breadth = coarse.shape
    expanded = jnp.broadcast_to(
        coarse[:, :, None, :, None, :, None],
        (comps, layers, factor, height, factor, breadth, factor),
    )
    return expanded.reshape(comps, layers * factor, height * factor, breadth * factor)


def paired_sums(residual, preconditioned, image):
    return lax.psum(
        (jnp.sum(residual * preconditioned), jnp.sum(preconditioned * image)), ("grp", "gz")
    )


def body(load, phases, clamp, phase_moduli):
    numbers = element_matrix()
    matrix = jnp.asarray(numbers, jnp.float32)
    bound = spectral_bound(numbers)
    omega = 1.2 / bound
    layers, height, breadth = phases.shape
    factor = COARSEN
    tile = lax.axis_index(("grp", "gz"))
    tiles = lax.axis_size(("grp", "gz"))
    member = lax.axis_index("gz")
    members = lax.axis_size("gz")
    depth = tile * layers + jnp.arange(layers, dtype=jnp.int32)[:, None, None]
    rows_at = jnp.arange(height, dtype=jnp.int32)[None, :, None]
    columns_at = jnp.arange(breadth, dtype=jnp.int32)[None, None, :]
    picked = jnp.zeros((layers, height, breadth), jnp.float32)
    for phase in range(PHASES):
        picked = picked + jnp.where(phases == phase, phase_moduli[phase], jnp.float32(0.0))
    outside = (depth == tiles * layers - 1) | (rows_at == height - 1) | (columns_at == breadth - 1)
    moduli = jnp.where(outside, jnp.float32(0.0), picked)
    free = jnp.where((depth == 0) & (clamp[None] == 1), 0.0, 1.0).astype(jnp.float32)
    lower = passed_along(moduli[-1:], ("grp", "gz"), 1)
    inverse = 1.0 / (free * node_diagonal(lower, moduli, matrix) + 1.0 - free)

    def stiffness(field):
        above = passed_along(field[:, :1], ("grp", "gz"), -1)
        total = element_forces(jnp.concatenate([field, above], 1), moduli, matrix)
        below = passed_along(total[:, -1:], ("grp", "gz"), 1)
        return total[:, :-1].at[:, :1].add(below)

    def operator(field):
        return free * stiffness(free * field) + (1.0 - free) * field

    coarse_layers = layers // factor
    coarse_height = height // factor
    coarse_breadth = breadth // factor
    group_layers = members * coarse_layers
    block_mean = moduli.reshape(
        coarse_layers, factor, coarse_height, factor, coarse_breadth, factor
    ).mean((1, 3, 5))
    coarse_depth = (
        member * coarse_layers + jnp.arange(coarse_layers, dtype=jnp.int32)[:, None, None]
    )
    coarse_rows = jnp.arange(coarse_height, dtype=jnp.int32)[None, :, None]
    coarse_columns = jnp.arange(coarse_breadth, dtype=jnp.int32)[None, None, :]
    coarse_edge = (
        (coarse_depth == group_layers - 1)
        | (coarse_rows == coarse_height - 1)
        | (coarse_columns == coarse_breadth - 1)
    )
    coarse_local = jnp.where(coarse_edge, jnp.float32(0.0), block_mean)
    group_moduli = lax.all_gather(coarse_local, "gz", axis=0, tiled=True)
    coarse_matrix = factor * matrix
    coarse_bottom = jnp.zeros((1, coarse_height, coarse_breadth), jnp.float32)
    coarse_top = jnp.zeros((3, 1, coarse_height, coarse_breadth), jnp.float32)
    coarse_inverse = 1.0 / node_diagonal(coarse_bottom, group_moduli, coarse_matrix)

    def coarse_apply(field):
        return element_forces(jnp.concatenate([field, coarse_top], 1), group_moduli, coarse_matrix)[
            :, :-1
        ]

    def solve_group(summed):
        return chebyshev(summed, coarse_apply, coarse_inverse, bound, CHEB)

    def blank_group(summed):
        return jnp.zeros_like(summed)

    def precondition(current):
        first = omega * current * inverse
        defect = current - operator(first)
        restricted = restrict(defect, factor)
        summed = lax.all_gather(restricted, "gz", axis=1, tiled=True)
        solved = lax.cond(member == 0, solve_group, blank_group, summed)
        solved = spread(solved, "gz", 0)
        own = lax.dynamic_slice_in_dim(solved, member * coarse_layers, coarse_layers, 1)
        second = first + free * prolong(own, factor)
        return second + omega * (current - operator(second)) * inverse

    rhs = free * load
    displacement = jnp.zeros_like(rhs)
    residual = rhs
    preconditioned = precondition(residual)
    image = operator(preconditioned)
    gamma, curve = paired_sums(residual, preconditioned, image)
    alpha = gamma / curve
    direction = preconditioned
    along = image
    for step in range(ITERS):
        displacement = displacement + alpha * direction
        residual = residual - alpha * along
        if step + 1 < ITERS:
            preconditioned = precondition(residual)
            image = operator(preconditioned)
            following, curve = paired_sums(residual, preconditioned, image)
            beta = following / gamma
            alpha = following / (curve - beta * following / alpha)
            direction = preconditioned + beta * direction
            along = image + beta * along
            gamma = following
    return (displacement, residual)


def solution(mesh):
    placed = (P(None, ("grp", "gz"), None, None), P(("grp", "gz"), None, None), P(), P())
    return jax.shard_map(
        body,
        mesh=mesh,
        in_specs=placed,
        out_specs=(P(None, ("grp", "gz"), None, None), P(None, ("grp", "gz"), None, None)),
        check_vma=False,
    )
```

profile of v0, /device:TPU:0, one launch (start us, length us, event | category | flops | bytes accessed | tf_op | source)
XLA Modules:
  0.0 781.7 jit_solution(1037202731570324370)
XLA Ops:
  2.2 3.6 fusion.298
  5.8 2.4 collective-permute-start
  8.7 12.1 %all_gather.9 = f32[8,8,16]{2,1,0:T(8,128)} all-gather(f32[1,8,16]{2,1,0:T(8,128)S(1)} %bitcast_select_fusion), channel_id=1, replica_groups=mesh['grp'=4,'gz'=8] {'gz'}, dimensions={0}, use_global_device_ids=true | all-gather | bytes 4608 | tf_op jit(solution)/shard_map/all_gather | solution.py:209
  36.3 44.2 %while.252 = (s32[]{:T(128)}, f32[3,9,64,128]{3,2,1,0:T(8,128)}, s32[2]{0:T(128)S(1)}, f32[3,9,64,128]{3,2,1,0:T(8,128)S(1)}, f32[8,64,128]{2,1,0:T(8,128)S(1)},...) while((s32[]{:T(128)}, f32[3,9,64,128]{3,2,1,0:T(8,128)}, ...), condition=%wide.region_3.4_spmd.clone, body=%wide.region_2.3_spmd.sunk.clone.sunk | while | flops 230057488 | bytes 52208232 | solution.py:102
  45.3 6.5 multiply_bitcast_fusion.12
  67.4 6.5 multiply_bitcast_fusion.12
  81.5 5.4 collective-permute-start.2
  86.9 1.9 add_divide_fusion
  92.5 9.1 %all-gather = f32[3,64,16]{2,1,0:T(8,128)S(1)} all-gather(f32[3,8,16]{2,1,0:T(8,128)S(1)} %reduce_sum.93), channel_id=2, replica_groups=mesh['grp'=4,'gz'=8] {'gz'}, dimensions={1}, use_global_device_ids=true | all-gather | bytes 13824 | tf_op jit(solution)/shard_map/all_gather | solution.py:230
  101.7 105.1 %conditional.2 = (f32[3,8,8,16]{3,2,0,1:T(8,128)}) conditional(s32[]{:T(128)} %convert_element_type.4, () %tuple.572, (f32[3,8,8,16]{0,3,2,1:T(8,128)S(1)}, f32[3,8,8,16]{3,2,1,0:T(8,128)S(1)}, f32[24,24]{1,0:T(8,128)S(1)}, f32[8,8,16]{2,1,0:T(8,128)}) %tuple.1309), branch_computations={%region_6.7_spmd, %region_7.14_spmd} | conditional | flops 10876638 | bytes 24754408 | solution.py:231
  104.3 30.9 %while.246 = (s32[]{:T(128)}, f32[3,9,8,16]{0,3,2,1:T(8,128)}, s32[2]{0:T(128)S(1)}, f32[3,9,8,16]{3,2,1,0:T(8,128)S(1)}, f32[24,24]{1,0:T(8,128)S(1)}, /*index=...) while((s32[]{:T(128)}, f32[3,9,8,16]{0,3,2,1:T(8,128)}, ...), condition=%wide.region_9.9_spmd, body=%wide.region_8.8_spmd.sunk | while | flops 3594826 | bytes 8055736 | solution.py:102
  118.0 1.8 add_dynamic-update-slice_fusion.53
  133.5 1.8 add_dynamic-update-slice_fusion.53
  138.7 30.9 %while.247 = (s32[]{:T(128)}, f32[3,9,8,16]{0,3,2,1:T(8,128)}, s32[2]{0:T(128)S(1)}, f32[3,9,8,16]{3,2,1,0:T(8,128)S(1)}, f32[24,24]{1,0:T(8,128)S(1)}, /*index=...) while((s32[]{:T(128)}, f32[3,9,8,16]{0,3,2,1:T(8,128)}, ...), condition=%wide.region_11.11_spmd, body=%wide.region_10.10_spmd.sunk | while | flops 3594826 | bytes 8055736 | solution.py:102
  152.4 1.8 add_dynamic-update-slice_fusion.56
  172.7 31.0 %while.248 = (s32[]{:T(128)}, f32[3,9,8,16]{0,3,2,1:T(8,128)}, s32[2]{0:T(128)S(1)}, f32[3,9,8,16]{3,2,1,0:T(8,128)S(1)}, f32[24,24]{1,0:T(8,128)S(1)}, /*index=...) while((s32[]{:T(128)}, f32[3,9,8,16]{0,3,2,1:T(8,128)}, ...), condition=%wide.region_13.13_spmd, body=%wide.region_12.12_spmd.sunk | while | flops 3594826 | bytes 8055736 | solution.py:102
  186.5 1.8 add_dynamic-update-slice_fusion.59
  202.0 1.8 add_dynamic-update-slice_fusion.59
  203.7 2.0 add_add_fusion
  207.8 23.2 %psum.42 = f32[3,8,8,16]{3,2,0,1:T(8,128)S(1)} all-reduce(f32[3,8,8,16]{3,2,0,1:T(8,128)S(1)} %broadcast_select_fusion.1), channel_id=1, replica_groups=mesh['grp'=4,'gz'=8] {'gz'}, use_global_device_ids=true, to_apply=%region_14.15 | all-reduce | flops 3072 | bytes 24576 | tf_op jit(solution)/shard_map/psum | solution.py:28
  232.3 2.1 broadcast_in_dim.72
  238.9 44.2 %while.253 = (s32[]{:T(128)}, f32[3,9,64,128]{3,2,1,0:T(8,128)}, s32[2]{0:T(128)S(1)}, f32[3,9,64,128]{3,2,1,0:T(8,128)S(1)}, f32[8,64,128]{2,1,0:T(8,128)S(1)},...) while((s32[]{:T(128)}, f32[3,9,64,128]{3,2,1,0:T(8,128)}, ...), condition=%wide.region_16.17_spmd.clone, body=%wide.region_15.16_spmd.sunk.clone.sunk | while | flops 230057488 | bytes 52208232 | solution.py:102
  247.9 6.5 multiply_bitcast_fusion.13
  270.1 6.5 multiply_bitcast_fusion.13
  284.0 2.9 collective-permute-start.4
  289.0 2.4 broadcast_multiply_fusion.2
  292.7 1.9 collective-permute-done.5
  295.7 44.2 %while.254 = (s32[]{:T(128)}, f32[3,9,64,128]{3,2,1,0:T(8,128)}, s32[2]{0:T(128)S(1)}, f32[3,9,64,128]{3,2,1,0:T(8,128)S(1)}, f32[8,64,128]{2,1,0:T(8,128)S(1)},...) while((s32[]{:T(128)}, f32[3,9,64,128]{3,2,1,0:T(8,128)}, ...), condition=%wide.region_20.21_spmd.clone, body=%wide.region_19.20_spmd.sunk.clone.sunk | while | flops 230057488 | bytes 52208232 | solution.py:102
  304.8 6.5 multiply_bitcast_fusion.14
  326.9 6.5 multiply_bitcast_fusion.14
  341.0 5.5 collective-permute-start.6
  348.6 2.5 multiply_reduce_fusion.2
  351.1 46.4 %all-reduce.20 = (f32[]{:T(128)}, f32[]{:T(128)}) all-reduce(f32[]{:T(128)} %get-tuple-element.2475, f32[]{:T(128)} %get-tuple-element.2474), channel_id=1, replica_groups=mesh['grp'=4,'gz'=8] {'grp','gz'}, use_global_device_ids=true, to_apply=%region_18.19 | all-reduce | flops 2 | bytes 16 | tf_op jit(solution)/shard_map/psum | solution.py:154
  398.8 2.4 fusion.284
  403.4 1.9 collective-permute-done.7
  407.5 44.5 %while.255 = (s32[]{:T(128)}, f32[3,9,64,128]{3,2,1,0:T(8,128)}, s32[2]{0:T(128)S(1)}, f32[3,9,64,128]{3,2,1,0:T(8,128)S(1)}, f32[8,64,128]{2,1,0:T(8,128)S(1)},...) while((s32[]{:T(128)}, f32[3,9,64,128]{3,2,1,0:T(8,128)}, ...), condition=%wide.region_24.25_spmd.clone, body=%wide.region_23.24_spmd.sunk.clone.sunk | while | flops 230057488 | bytes 52208232 | solution.py:102
  416.6 6.5 multiply_bitcast_fusion.15
  438.9 6.5 multiply_bitcast_fusion.15
  452.9 5.7 collective-permute-start.8
  462.3 2.0 reduce_sum.98
  465.8 11.1 %all-gather.1 = f32[3,64,16]{2,1,0:T(8,128)S(1)} all-gather(f32[3,8,16]{2,1,0:T(8,128)S(1)} %reduce_sum.99), channel_id=3, replica_groups=mesh['grp'=4,'gz'=8] {'gz'}, dimensions={1}, use_global_device_ids=true | all-gather | bytes 13824 | tf_op jit(solution)/shard_map/all_gather | solution.py:230
  477.0 105.4 %conditional.3 = (f32[3,8,8,16]{3,2,0,1:T(8,128)}) conditional(s32[]{:T(128)} %convert_element_type.4, () %tuple.577, (f32[3,8,8,16]{0,3,2,1:T(8,128)S(1)}, f32[3,8,8,16]{3,2,1,0:T(8,128)S(1)}, f32[24,24]{1,0:T(8,128)S(1)}, f32[8,8,16]{2,1,0:T(8,128)}) %tuple.1308), branch_computations={%region_27.28_spmd, %region_28.35_spmd} | conditional | flops 10876638 | bytes 24754408 | solution.py:231
  479.6 30.8 %while.249 = (s32[]{:T(128)}, f32[3,9,8,16]{0,3,2,1:T(8,128)}, s32[2]{0:T(128)S(1)}, f32[3,9,8,16]{3,2,1,0:T(8,128)S(1)}, f32[24,24]{1,0:T(8,128)S(1)}, /*index=...) while((s32[]{:T(128)}, f32[3,9,8,16]{0,3,2,1:T(8,128)}, ...), condition=%wide.region_30.30_spmd, body=%wide.region_29.29_spmd.sunk | while | flops 3594826 | bytes 8055736 | solution.py:102
  493.2 1.8 add_dynamic-update-slice_fusion.44
  513.9 31.2 %while.250 = (s32[]{:T(128)}, f32[3,9,8,16]{0,3,2,1:T(8,128)}, s32[2]{0:T(128)S(1)}, f32[3,9,8,16]{3,2,1,0:T(8,128)S(1)}, f32[24,24]{1,0:T(8,128)S(1)}, /*index=...) while((s32[]{:T(128)}, f32[3,9,8,16]{0,3,2,1:T(8,128)}, ...), condition=%wide.region_32.32_spmd, body=%wide.region_31.31_spmd.sunk | while | flops 3594826 | bytes 8055736 | solution.py:102
  527.7 1.8 add_dynamic-update-slice_fusion.47
  543.3 1.8 add_dynamic-update-slice_fusion.47
  548.1 31.2 %while.251 = (s32[]{:T(128)}, f32[3,9,8,16]{0,3,2,1:T(8,128)}, s32[2]{0:T(128)S(1)}, f32[3,9,8,16]{3,2,1,0:T(8,128)S(1)}, f32[24,24]{1,0:T(8,128)S(1)}, /*index=...) while((s32[]{:T(128)}, f32[3,9,8,16]{0,3,2,1:T(8,128)}, ...), condition=%wide.region_34.34_spmd, body=%wide.region_33.33_spmd.sunk | while | flops 3594826 | bytes 8055736 | solution.py:102
  561.9 1.8 add_dynamic-update-slice_fusion.50
  579.3 2.0 add_add_fusion.1
  583.3 23.2 %psum.45 = f32[3,8,8,16]{3,2,0,1:T(8,128)S(1)} all-reduce(f32[3,8,8,16]{3,2,0,1:T(8,128)S(1)} %broadcast_select_fusion), channel_id=1, replica_groups=mesh['grp'=4,'gz'=8] {'gz'}, use_global_device_ids=true, to_apply=%region_35.36 | all-reduce | flops 3072 | bytes 24576 | tf_op jit(solution)/shard_map/psum | solution.py:28
  607.8 2.1 broadcast_in_dim.77
  614.4 44.4 %while.256 = (s32[]{:T(128)}, f32[3,9,64,128]{3,2,1,0:T(8,128)}, s32[2]{0:T(128)S(1)}, f32[3,9,64,128]{3,2,1,0:T(8,128)S(1)}, f32[8,64,128]{2,1,0:T(8,128)S(1)},...) while((s32[]{:T(128)}, f32[3,9,64,128]{3,2,1,0:T(8,128)}, ...), condition=%wide.region_37.38_spmd.clone, body=%wide.region_36.37_spmd.sunk.clone.sunk | while | flops 230057488 | bytes 52208232 | solution.py:102
  623.6 6.5 multiply_bitcast_fusion.16
  645.8 6.5 multiply_bitcast_fusion.16
  659.8 2.5 collective-permute-start.10
  664.4 2.4 broadcast_multiply_fusion.3
  671.1 44.4 %while.257 = (s32[]{:T(128)}, f32[3,9,64,128]{3,2,1,0:T(8,128)}, s32[2]{0:T(128)S(1)}, f32[3,9,64,128]{3,2,1,0:T(8,128)S(1)}, f32[8,64,128]{2,1,0:T(8,128)S(1)},...) while((s32[]{:T(128)}, f32[3,9,64,128]{3,2,1,0:T(8,128)}, ...), condition=%wide.region_41.42_spmd.clone, body=%wide.region_40.41_spmd.sunk.clone.sunk | while | flops 230057488 | bytes 52208232 | solution.py:102
  680.2 6.5 multiply_bitcast_fusion.17
  702.5 6.5 multiply_bitcast_fusion.17
  716.6 5.7 collective-permute-start.12
  725.3 2.1 multiply_reduce_fusion
  727.4 46.4 %all-reduce.19 = (f32[]{:T(128)}, f32[]{:T(128)}) all-reduce(f32[]{:T(128)} %get-tuple-element.2477, f32[]{:T(128)} %get-tuple-element.2476), channel_id=1, replica_groups=mesh['grp'=4,'gz'=8] {'grp','gz'}, use_global_device_ids=true, to_apply=%region_39.40 | all-reduce | flops 2 | bytes 16 | tf_op jit(solution)/shard_map/psum | solution.py:154
  778.4 3.0 multiply_subtract_fusion
  (1299 shorter events, 423.2 us)
Async XLA Ops:
  0.6 26.0 %copy-start.16 = (f32[24,24]{1,0:T(8,128)S(1)}, f32[24,24]{1,0:T(8,128)}, u32[]{:S(2)}) copy-start(f32[24,24]{1,0:T(8,128)} %constant.3032.clone) | copy-start | bytes 6916
  0.6 27.4 %copy-start = (f32[24,24]{1,0:T(8,128)S(1)}, f32[24,24]{1,0:T(8,128)}, u32[]{:S(2)}) copy-start(f32[24,24]{1,0:T(8,128)} %constant.3073) | copy-start | bytes 6916
  5.8 24.0 %collective-permute-start = (f32[1,64,128]{2,1,0:T(8,128)S(1)}, f32[1,64,128]{2,1,0:T(8,128)S(1)}, u32[]{:S(2)}, u32[]{:S(2)}) collective-permute-start(f32[1,64,128]{2,1,0:T(8,128)S(1)} %slice.6742), channel_id=1, source_target_pairs={{0,1},{1,2},{2,3},{3,4},{4,5},{5,6},{6,7},{7,8},{8,9},{9,10},{10,1... | collective-permute-start | bytes 98312 | tf_op jit(solution)/shard_map/ppermute | solution.py:23
  29.6 61.6 %copy-start.17 = (f32[8,64,128]{2,1,0:T(8,128)}, f32[8,64,128]{2,1,0:T(8,128)S(1)}, u32[]{:S(2)}) copy-start(f32[8,64,128]{2,1,0:T(8,128)S(1)} %get-tuple-element.2978) | copy-start | bytes 786436
  30.9 2.6 copy-start.69
  31.3 5.0 copy-start.37
  32.0 3.2 collective-permute-start.1
  36.3 50.6 %copy-start.70 = (f32[3]{0:T(128)S(1)}, f32[3]{0:T(128)}, u32[]{:S(2)}) copy-start(f32[3]{0:T(128)} %get-tuple-element.2986) | copy-start | bytes 40
  36.3 50.6 %copy-start.71 = (f32[3]{0:T(128)S(1)}, f32[3]{0:T(128)}, u32[]{:S(2)}) copy-start(f32[3]{0:T(128)} %get-tuple-element.2987) | copy-start | bytes 40
  80.5 10.7 %copy-start.5 = (f32[3,8,64,128]{3,2,1,0:T(8,128)S(1)}, f32[3,8,64,128]{3,2,1,0:T(8,128)}, u32[]{:S(2)}) copy-start(f32[3,8,64,128]{3,2,1,0:T(8,128)} %param.237) | copy-start | bytes 2359300
  81.5 8.8 %collective-permute-start.2 = (f32[3,1,64,128]{3,2,1,0:T(8,128)S(1)}, f32[3,1,64,128]{3,2,1,0:T(8,128)S(1)}, u32[]{:S(2)}, u32[]{:S(2)}) collective-permute-start(f32[3,1,64,128]{3,2,1,0:T(8,128)S(1)} %slice.5989), channel_id=1, source_target_pairs={{0,1},{1,2},{2,3},{3,4},{4,5},{5,6},{6,7},{7,8},{8,9},{9,10},{10,1... | collective-permute-start | bytes 294920 | tf_op jit(solution)/shard_map/ppermute | solution.py:23
  88.8 12.9 %copy-start.2 = (f32[3,8,8,16]{0,3,2,1:T(8,128)}, f32[3,8,8,16]{0,3,2,1:T(8,128)S(1)}, u32[]{:S(2)}) copy-start(f32[3,8,8,16]{0,3,2,1:T(8,128)S(1)} %add_divide_fusion) | copy-start | bytes 36868
  115.0 2.1 copy-start.43
  115.8 1.5 copy-start.63
  115.8 2.1 copy-start.44
  130.4 2.1 copy-start.43
  131.3 1.5 copy-start.63
  131.3 2.1 copy-start.44
  149.4 2.1 copy-start.45
  150.2 2.1 copy-start.46
  164.9 2.1 copy-start.45
  165.7 2.1 copy-start.46
  183.5 2.1 copy-start.47
  184.3 2.1 copy-start.48
  199.0 2.1 copy-start.47
  199.8 1.5 copy-start.65
  199.8 2.1 copy-start.48
  206.8 27.6 %copy-start.6 = (f32[3,8,64,128]{3,2,1,0:T(8,128)S(1)}, f32[3,8,64,128]{3,2,1,0:T(8,128)}, u32[]{:S(2)}) copy-start(f32[3,8,64,128]{3,2,1,0:T(8,128)} %param.237) | copy-start | bytes 2359300
  234.4 4.5 copy-start.38
  234.6 3.2 collective-permute-start.3
  238.9 50.1 %copy-start.18 = (f32[8,64,128]{2,1,0:T(8,128)S(1)}, f32[8,64,128]{2,1,0:T(8,128)}, u32[]{:S(2)}) copy-start(f32[8,64,128]{2,1,0:T(8,128)} %copy-done.17) | copy-start | bytes 786436
  284.0 4.1 collective-permute-start.4
  291.4 3.2 collective-permute-start.5
  340.0 58.8 %copy-start.7 = (f32[3,8,64,128]{3,2,1,0:T(8,128)S(1)}, f32[3,8,64,128]{3,2,1,0:T(8,128)}, u32[]{:S(2)}) copy-start(f32[3,8,64,128]{3,2,1,0:T(8,128)} %param.237) | copy-start | bytes 2359300
  341.0 6.7 collective-permute-start.6
  348.6 52.6 %copy-start.34 = (f32[3,8,64,128]{3,2,1,0:T(8,128)}, f32[3,8,64,128]{3,2,1,0:T(8,128)S(1)}, u32[]{:S(2)}) copy-start(f32[3,8,64,128]{3,2,1,0:T(8,128)S(1)} %add_dynamic-update-slice_fusion.21) | copy-start | bytes 2359300
  402.1 3.2 collective-permute-start.7
  451.9 12.3 %copy-start.39 = (f32[24,24,1,1]{1,0,3,2:T(8,128)}, f32[24,24,1,1]{1,0,3,2:T(8,128)S(1)}, u32[]{:S(2)}) copy-start(f32[24,24,1,1]{1,0,3,2:T(8,128)S(1)} %get-tuple-element.4566) | copy-start | bytes 6916
  452.9 6.9 collective-permute-start.8
  460.7 16.2 %copy-start.1 = (f32[24,24]{1,0:T(8,128)S(1)}, f32[24,24]{1,0:T(8,128)}, u32[]{:S(2)}) copy-start(f32[24,24]{1,0:T(8,128)} %constant.3073) | copy-start | bytes 6916
  460.7 16.2 %copy-start.3 = (f32[3,8,8,16]{0,3,2,1:T(8,128)S(1)}, f32[3,8,8,16]{0,3,2,1:T(8,128)}, u32[]{:S(2)}) copy-start(f32[3,8,8,16]{0,3,2,1:T(8,128)} %copy-done.2) | copy-start | bytes 36868
  490.2 2.1 copy-start.49
  491.1 2.1 copy-start.50
  505.6 2.1 copy-start.49
  506.5 2.1 copy-start.50
  524.7 2.1 copy-start.51
  525.5 1.5 copy-start.67
  525.5 2.1 copy-start.52
  540.2 2.1 copy-start.51
  541.1 2.1 copy-start.52
  558.9 2.1 copy-start.53
  559.8 2.1 copy-start.54
  574.5 2.1 copy-start.53
  575.4 2.1 copy-start.54
  582.3 27.6 %copy-start.8 = (f32[3,8,64,128]{3,2,1,0:T(8,128)S(1)}, f32[3,8,64,128]{3,2,1,0:T(8,128)}, u32[]{:S(2)}) copy-start(f32[3,8,64,128]{3,2,1,0:T(8,128)} %get-tuple-element.2665) | copy-start | bytes 2359300
  609.9 4.5 copy-start.40
  610.1 3.2 collective-permute-start.9
  614.4 49.9 %copy-start.19 = (f32[8,64,128]{2,1,0:T(8,128)S(1)}, f32[8,64,128]{2,1,0:T(8,128)}, u32[]{:S(2)}) copy-start(f32[8,64,128]{2,1,0:T(8,128)} %copy-done.17) | copy-start | bytes 786436
  659.8 3.7 collective-permute-start.10
  666.8 3.2 collective-permute-start.11
  671.1 54.2 %copy-start.9 = (f32[3,8,64,128]{3,2,1,0:T(8,128)S(1)}, f32[3,8,64,128]{3,2,1,0:T(8,128)}, u32[]{:S(2)}) copy-start(f32[3,8,64,128]{3,2,1,0:T(8,128)} %get-tuple-element.2665) | copy-start | bytes 2359300
  715.6 62.8 %copy-start.35 = (f32[3,8,64,128]{3,2,1,0:T(8,128)S(1)}, f32[3,8,64,128]{3,2,1,0:T(8,128)}, u32[]{:S(2)}) copy-start(f32[3,8,64,128]{3,2,1,0:T(8,128)} %copy-done.34) | copy-start | bytes 2359300
  715.6 62.8 %copy-start.36 = (f32[3,8,64,128]{3,2,1,0:T(8,128)S(1)}, f32[3,8,64,128]{3,2,1,0:T(8,128)}, u32[]{:S(2)}) copy-start(f32[3,8,64,128]{3,2,1,0:T(8,128)} %get-tuple-element.2667) | copy-start | bytes 2359300
  716.6 6.9 collective-permute-start.12
  (71 other events, 74.8 us)
where the time goes:
time: 792 us; the launch traced here: 782 us
  other arithmetic  226 us (29%)
  local copies, waits for them, and re-layouts  217 us (27%)
  blocking collectives  171 us (22%)
  matrix products  89.6 us (11%)
  starting transfers between devices  38.5 us (5%)
  loops' own time  20.7 us (3%)
  waiting for transfers between devices  10.6 us (1%)
    psum x2, blocking collectives, paired_sums(): lax.psum((jnp.sum(residual * preconditioned), jnp.sum(preconditioned * im...  92.8 us
    dot_general x24, matrix products, add_block(): jnp.einsum('ij,jzyx->izyx', matrix, gathered, precision=lax.Precision.HIG...  89.6 us
    slice x144, local copies, waits for them, and re-layouts, add_block(): jnp.roll(forces[corner], (offset[1], offset[2]), (2, 3))  72.7 us
    while x120, other arithmetic  55.6 us
    scatter-add x144, other arithmetic, add_block(): update.at[:, offset[0]:offset[0] + width]  55.2 us
    psum x2, blocking collectives, spread(): return lax.psum(block, axis)  46.3 us
    ppermute x13, starting transfers between devices, passed_along(): return lax.ppermute(value, axis, pairs)  38.5 us
    while x216, local copies, waits for them, and re-layouts  37.6 us
  transfers between devices with their start and end apart: 13, of which 6 were waited for; matrix products, arithmetic and copies ran while one was open for 2% of the time, Pallas kernels for 0%

commit v1 on v0

v1 whole, which is shorter than its diff:
```python
import functools
import math

import jax
import jax.numpy as jnp
import numpy as np
from jax import lax
from jax.experimental import pallas as pl
from jax.experimental.pallas import tpu as pltpu
from jax.sharding import PartitionSpec as P

PHASES = 4
COARSEN = 8
CHEB = 4
ITERS = 2
HALO = 2
MESH = pl.DeviceIdType.MESH

POISSON = 0.3
LAME = POISSON / ((1.0 + POISSON) * (1.0 - 2.0 * POISSON))
SHEAR = 1.0 / (2.0 * (1.0 + POISSON))


CORNER_OFFSETS = [
    (along_z, along_y, along_x) for along_z in (0, 1) for along_y in (0, 1) for along_x in (0, 1)
]


def element_matrix():
    elastic = np.zeros((6, 6))
    elastic[:3, :3] = LAME
    for axis_one in range(3):
        elastic[axis_one, axis_one] = LAME + 2.0 * SHEAR
        elastic[axis_one + 3, axis_one + 3] = SHEAR
    points = [0.5 - 0.5 / math.sqrt(3.0), 0.5 + 0.5 / math.sqrt(3.0)]
    pairs = [(0, 1), (1, 2), (0, 2)]
    matrix = np.zeros((24, 24))
    for first_point in points:
        for second_point in points:
            for third_point in points:
                spot = (first_point, second_point, third_point)
                strain = np.zeros((6, 24))
                for corner, offset in enumerate(CORNER_OFFSETS):
                    values = [
                        spot[axis_one] if offset[axis_one] else 1.0 - spot[axis_one]
                        for axis_one in range(3)
                    ]
                    slopes = [1.0 if offset[axis_one] else -1.0 for axis_one in range(3)]
                    slants = []
                    for axis_one in range(3):
                        others = [values[axis_two] for axis_two in range(3) if axis_two != axis_one]
                        slants.append(slopes[axis_one] * others[0] * others[1])
                        strain[axis_one, 3 * corner + axis_one] = slants[axis_one]
                    for position, pair in enumerate(pairs):
                        strain[3 + position, 3 * corner + pair[0]] = slants[pair[1]]
                        strain[3 + position, 3 * corner + pair[1]] = slants[pair[0]]
                matrix = matrix + 0.125 * (strain.T @ elastic @ strain)
    return matrix


def spectral_bound(numbers):
    diagonal_part = np.array([numbers[index, index] for index in range(numbers.shape[0])])
    return float(np.max(np.sum(np.abs(numbers), axis=1) / diagonal_part))


def voxel_forces(below, above, mod, scale):
    one, two, three = scale / 16.0, scale / 48.0, scale / 144.0
    u = []
    for k in range(3):
        modes = {}
        for b in (0, 1):
            for c in (0, 1):
                if b or c:
                    modes[(0, b, c)] = below[k][b][c] + above[k][b][c]
                modes[(1, b, c)] = above[k][b][c] - below[k][b][c]
        u.append(modes)
    unit = [(1, 0, 0), (0, 1, 0), (0, 0, 1)]

    def pair(i, j):
        return tuple(unit[i][d] + unit[j][d] for d in range(3))

    f = [{}, {}, {}]
    trace = (mod * (one * LAME)) * (u[0][unit[0]] + u[1][unit[1]] + u[2][unit[2]])
    stretch = mod * (2.0 * one * SHEAR)
    slide = mod * (one * SHEAR)
    for k in range(3):
        f[k][unit[k]] = trace + stretch * u[k][unit[k]]
    for i, j in ((0, 1), (1, 2), (0, 2)):
        shear = slide * (u[i][unit[j]] + u[j][unit[i]])
        f[i][unit[j]] = shear
        f[j][unit[i]] = shear
    same = mod * (two * (LAME + 3.0 * SHEAR))
    cross = mod * (two * LAME)
    for k in range(3):
        for m in range(3):
            if m != k:
                j = 3 - k - m
                f[k][pair(k, m)] = same * u[k][pair(k, m)] + cross * u[j][pair(j, m)]
    twist = mod * (two * SHEAR)
    total = u[0][pair(1, 2)] + u[1][pair(0, 2)] + u[2][pair(0, 1)]
    for k in range(3):
        i, j = [d for d in range(3) if d != k]
        f[k][pair(i, j)] = twist * (u[k][pair(i, j)] + total)
    warp = mod * (three * (LAME + 4.0 * SHEAR))
    for k in range(3):
        f[k][(1, 1, 1)] = warp * u[k][(1, 1, 1)]
    low = [[[None, None], [None, None]] for k in range(3)]
    high = [[[None, None], [None, None]] for k in range(3)]
    for k in range(3):
        for b in (0, 1):
            for c in (0, 1):
                if b or c:
                    low[k][b][c] = f[k][(0, b, c)] - f[k][(1, b, c)]
                    high[k][b][c] = f[k][(0, b, c)] + f[k][(1, b, c)]
                else:
                    low[k][b][c] = -f[k][(1, b, c)]
                    high[k][b][c] = f[k][(1, b, c)]
    return low, high


def plane_modes(value, ahead_y, ahead_x):
    shifted = ahead_x(value)
    rows = [value + shifted, shifted - value]
    out = [[None, None], [None, None]]
    for c in (0, 1):
        up = ahead_y(rows[c])
        out[0][c] = rows[c] + up
        out[1][c] = up - rows[c]
    return out


def plane_forces(force, behind_y, behind_x):
    rows = [
        (force[0][c] - force[1][c]) + behind_y(force[0][c] + force[1][c]) for c in (0, 1)
    ]
    return (rows[0] - rows[1]) + behind_x(rows[0] + rows[1])


def kernel(
    groups,
    members,
    load,
    phases,
    clamp,
    phase_moduli,
    out_u,
    out_r,
    R,
    S,
    W,
    MOD,
    PH,
    FREE,
    PRO,
    FWD,
    FSUM,
    CARRY,
    ACC,
    STAGE,
    GAT,
    DOT,
    DSUM,
    DOTG,
    halo_send,
    halo_recv,
    gat_send,
    gat_recv,
    cross_send,
    cross_recv,
    dot_send,
    dot_recv,
    dotg_send,
    dotg_recv,
):
    numbers = element_matrix()
    entry = float(numbers[0, 0])
    bound = spectral_bound(numbers)
    omega = 1.2 / bound
    _, layers, height, breadth = load.shape
    coarse_height = height // COARSEN
    coarse_breadth = breadth // COARSEN
    grp = lax.axis_index("grp")
    me = lax.axis_index("gz")
    tile = grp * members + me
    tiles = groups * members
    has_below = tile > 0
    has_above = tile < tiles - 1

    GAT[...] = jnp.zeros(GAT.shape, jnp.float32)
    barrier = pltpu.get_barrier_semaphore()

    def greet(o, unused):
        other = lax.rem(tile + o, tiles)
        pl.semaphore_signal(
            barrier,
            inc=1,
            device_id=(other // members, lax.rem(other, members)),
            device_id_type=MESH,
        )
        return unused

    lax.fori_loop(1, tiles, greet, 0)

    rows_at = lax.broadcasted_iota(jnp.int32, (height, breadth), 0)
    columns_at = lax.broadcasted_iota(jnp.int32, (height, breadth), 1)
    inside = (rows_at < height - 1) & (columns_at < breadth - 1)

    def moduli_of(labels, depth):
        picked = jnp.zeros((height, breadth), jnp.float32)
        for phase in range(PHASES):
            picked = jnp.where(labels == phase, phase_moduli[phase], picked)
        keep = jnp.where((depth >= 0) & (depth < tiles * layers - 1), 1.0, 0.0)
        return jnp.where(inside, picked, 0.0) * keep

    first_depth = tile * layers
    bottom = jnp.where(tile == 0, 1.0, 0.0)
    held = jnp.where(clamp[...] == 1, 1.0, 0.0) * bottom
    FREE[0] = 1.0 - held
    FREE[1] = jnp.ones((height, breadth), jnp.float32)

    ACC[0] = jnp.zeros((height, breadth), jnp.float32)

    def own_layer(n, unused):
        mod = moduli_of(phases[n], first_depth + n)
        MOD[n + 3] = mod
        ACC[0] = ACC[0] + mod
        free = FREE[jnp.where(n == 0, 0, 1)]
        for k in range(3):
            R[0, k, n + HALO] = free * load[k, n]
        return unused

    lax.fori_loop(0, layers, own_layer, 0)

    @pl.when(tile == 0)
    def _():
        PH[0:3] = jnp.zeros((3, height, breadth), jnp.int32)
        for it in range(2):
            R[it, :, 0:HALO] = jnp.zeros((3, HALO, height, breadth), jnp.float32)

    @pl.when(tile == tiles - 1)
    def _():
        PH[3:5] = jnp.zeros((2, height, breadth), jnp.int32)
        for it in range(2):
            R[it, :, layers + HALO :] = jnp.zeros((3, HALO, height, breadth), jnp.float32)

    STAGE[...] = jnp.zeros(STAGE.shape, jnp.float32)

    pl.semaphore_wait(barrier, tiles - 1)

    above_tile = jnp.minimum(tile + 1, tiles - 1)
    below_tile = jnp.maximum(tile - 1, 0)
    above_id = (above_tile // members, lax.rem(above_tile, members))
    below_id = (below_tile // members, lax.rem(below_tile, members))

    def to_above(src, dst, index):
        return pltpu.make_async_remote_copy(
            src_ref=src,
            dst_ref=dst,
            send_sem=halo_send.at[index],
            recv_sem=halo_recv.at[index],
            device_id=above_id,
            device_id_type=MESH,
        )

    def to_below(src, dst, index):
        return pltpu.make_async_remote_copy(
            src_ref=src,
            dst_ref=dst,
            send_sem=halo_send.at[index],
            recv_sem=halo_recv.at[index],
            device_id=below_id,
            device_id_type=MESH,
        )

    def field_up(it, depth):
        return to_above(
            R.at[it, :, HALO + layers - 1 - depth],
            R.at[it, :, HALO - 1 - depth],
            2 + it * 4 + depth,
        )

    def field_down(it, depth):
        return to_below(
            R.at[it, :, HALO + depth], R.at[it, :, HALO + layers + depth], 4 + it * 4 + depth
        )

    phases_up = to_above(phases.at[layers - 3 : layers], PH.at[0:3], 0)
    phases_down = to_below(phases.at[0:2], PH.at[3:5], 1)

    def start_field(it):
        for depth in range(HALO):

            @pl.when(has_above)
            def _():
                field_up(it, depth).start()

            @pl.when(has_below)
            def _():
                field_down(it, depth).start()

    def wait_field(it, depth):
        @pl.when(has_above)
        def _():
            field_up(it, depth).wait_send()
            field_down(it, depth).wait_recv()

        @pl.when(has_below)
        def _():
            field_down(it, depth).wait_send()
            field_up(it, depth).wait_recv()

    @pl.when(has_above)
    def _():
        phases_up.start()

    @pl.when(has_below)
    def _():
        phases_down.start()

    start_field(0)

    lanes = coarse_height * coarse_breadth
    fine_at = lax.broadcasted_iota(jnp.int32, (breadth, lanes), 0)
    lane_at = lax.broadcasted_iota(jnp.int32, (breadth, lanes), 1)
    gather_x = jnp.where(
        fine_at // COARSEN == lax.rem(lane_at, coarse_breadth), 1.0, 0.0
    ).astype(jnp.float32)
    coarse_at = lax.broadcasted_iota(jnp.int32, (lanes, breadth), 0)
    column_at = lax.broadcasted_iota(jnp.int32, (lanes, breadth), 1)
    spread_x = jnp.where(
        lax.rem(coarse_at, coarse_breadth) == column_at // COARSEN, 1.0, 0.0
    ).astype(jnp.float32)
    row_mask = jnp.where(
        lax.broadcasted_iota(jnp.int32, (coarse_height, lanes), 0)
        == lax.broadcasted_iota(jnp.int32, (coarse_height, lanes), 1) // coarse_breadth,
        1.0,
        0.0,
    ).astype(jnp.float32)

    def block_row(plane):
        summed = jnp.sum(plane.reshape(coarse_height, COARSEN, breadth), axis=1)
        wide = jnp.dot(
            summed, gather_x, precision=lax.Precision.HIGHEST, preferred_element_type=jnp.float32
        )
        return jnp.sum(wide * row_mask, axis=0, keepdims=True)

    def block_plane(row):
        wide = jnp.broadcast_to(row, (coarse_height, lanes)) * row_mask
        narrow = jnp.dot(
            wide, spread_x, precision=lax.Precision.HIGHEST, preferred_element_type=jnp.float32
        )
        return jnp.broadcast_to(
            narrow[:, None, :], (coarse_height, COARSEN, breadth)
        ).reshape(height, breadth)

    lane_row = lax.broadcasted_iota(jnp.int32, (1, lanes), 1)
    coarse_keep = (
        (lane_row // coarse_breadth < coarse_height - 1)
        & (lax.rem(lane_row, coarse_breadth) < coarse_breadth - 1)
    )
    in_group = jnp.where(me < members - 1, 1.0 / (COARSEN**3), 0.0)
    coarse_row = jnp.where(coarse_keep, block_row(ACC[0]), 0.0) * in_group
    for it in range(2):
        STAGE[it, 3:4] = coarse_row

    @pl.when(has_above)
    def _():
        phases_up.wait_send()
        phases_down.wait_recv()

    @pl.when(has_below)
    def _():
        phases_down.wait_send()
        phases_up.wait_recv()

    for n in range(3):
        MOD[n] = moduli_of(PH[n], first_depth - 3 + n)
    for n in range(2):
        MOD[layers + 3 + n] = moduli_of(PH[3 + n], first_depth + layers + n)

    def back_x(value):
        return pltpu.roll(value, 1, 1)

    def back_y(value):
        return pltpu.roll(value, 1, 0)

    def fore_x(value):
        return pltpu.roll(value, breadth - 1, 1)

    def fore_y(value):
        return pltpu.roll(value, height - 1, 0)

    def free_at(n):
        return FREE[jnp.where(n == 0, 0, 1)]

    def inverse_layer(i, unused):
        pair = MOD[i] + MOD[i + 1]
        pair = pair + back_x(pair)
        pair = pair + back_y(pair)
        free = free_at(i - HALO)
        depth = first_depth + i - HALO
        valid = (depth >= 0) & (depth < tiles * layers)
        diagonal = jnp.where(valid, free * (entry * pair) + 1.0 - free, 1.0)
        W[i] = omega / diagonal
        return unused

    lax.fori_loop(0, layers + 2 * HALO, inverse_layer, 0)

    def modes_into(get, n):
        slot = lax.rem(n + 4, 2)
        free = free_at(n)
        for k in range(3):
            modes = plane_modes(free * get(k, n), fore_y, fore_x)
            for b in (0, 1):
                for c in (0, 1):
                    FWD[slot, 4 * k + 2 * b + c] = modes[b][c]

    def apply_stiffness(get, put, lowest, highest):
        modes_into(get, jnp.int32(lowest - 1))
        CARRY[...] = jnp.zeros(CARRY.shape, jnp.float32)

        def layer(v, unused):
            modes_into(get, v + 1)
            lower = lax.rem(v + 4, 2)
            upper = lax.rem(v + 5, 2)

            def chunk(j, nothing):
                rows = pl.ds(pl.multiple_of(j * 8, 8), 8)

                def of(slot):
                    return [
                        [[FWD[slot, 4 * k + 2 * b + c, rows] for c in (0, 1)] for b in (0, 1)]
                        for k in range(3)
                    ]

                low, high = voxel_forces(of(lower), of(upper), MOD[v + 3, rows], 1.0)
                for k in range(3):
                    for b in (0, 1):
                        for c in (0, 1):
                            index = 4 * k + 2 * b + c
                            FSUM[index, rows] = CARRY[index, rows] + low[k][b][c]
                            CARRY[index, rows] = high[k][b][c]
                return nothing

            lax.fori_loop(0, height // 8, chunk, 0, unroll=True)

            @pl.when(v >= lowest)
            def _():
                free = free_at(v)
                for k in range(3):
                    force = [[FSUM[4 * k + 2 * b + c] for c in (0, 1)] for b in (0, 1)]
                    total = plane_forces(force, back_y, back_x)
                    put(k, v, free * total + (1.0 - free) * get(k, v))

            return unused

        lax.fori_loop(lowest - 1, highest + 1, layer, 0)

    def coarse_ahead(value, by):
        return pltpu.roll(value, lanes - by, 2)

    def coarse_behind(value, by):
        return pltpu.roll(value, by, 2)

    def coarse_apply(field, mod):
        fore = (
            functools.partial(coarse_ahead, by=coarse_breadth),
            functools.partial(coarse_ahead, by=1),
        )
        back = (
            functools.partial(coarse_behind, by=coarse_breadth),
            functools.partial(coarse_behind, by=1),
        )
        below = [plane_modes(field[k], *fore) for k in range(3)]
        above = [
            [[pltpu.roll(below[k][b][c], members - 1, 1) for c in (0, 1)] for b in (0, 1)]
            for k in range(3)
        ]
        low, high = voxel_forces(below, above, mod, float(COARSEN))
        out = []
        for k in range(3):
            force = [
                [low[k][b][c] + pltpu.roll(high[k][b][c], 1, 1) for c in (0, 1)] for b in (0, 1)
            ]
            out.append(plane_forces(force, *back))
        return out

    def coarse_solve(it):
        mod = GAT[it, :, :, 3, :]
        rhs = [GAT[it, :, :, k, :] for k in range(3)]
        pair = mod + pltpu.roll(mod, 1, 1)
        pair = pair + coarse_behind(pair, 1)
        pair = pair + coarse_behind(pair, coarse_breadth)
        diagonal = (COARSEN * entry) * pair
        present = diagonal > 0.0
        inverse = jnp.where(present, 1.0 / jnp.where(present, diagonal, 1.0), 0.0)
        low_end = bound / 20.0
        center = 0.5 * (bound + low_end)
        radius = 0.5 * (bound - low_end)
        sigma = center / radius
        rho = 1.0 / sigma
        update = [inverse * rhs[k] * (1.0 / center) for k in range(3)]
        correction = update
        remainder = rhs
        for sweep in range(CHEB - 1):
            image = coarse_apply(update, mod)
            remainder = [remainder[k] - image[k] for k in range(3)]
            rho_next = 1.0 / (2.0 * sigma - rho)
            update = [
                (rho_next * rho) * update[k] + (2.0 * rho_next / radius) * (inverse * remainder[k])
                for k in range(3)
            ]
            correction = [correction[k] + update[k] for k in range(3)]
            rho = rho_next
        return correction

    def peer_copy(it, o, src):
        other = lax.rem(me + o, members)
        return pltpu.make_async_remote_copy(
            src_ref=src,
            dst_ref=GAT.at[it, 0, me],
            send_sem=gat_send.at[it, o],
            recv_sem=gat_recv.at[it, me],
            device_id=(grp, other),
            device_id_type=MESH,
        )

    def peer_arrival(it, sender):
        return pltpu.make_async_remote_copy(
            src_ref=STAGE.at[it],
            dst_ref=GAT.at[it, 0, sender],
            send_sem=gat_send.at[it, 0],
            recv_sem=gat_recv.at[it, sender],
            device_id=(grp, sender),
            device_id_type=MESH,
        )

    def cross_copy(it, side, sender, target):
        return pltpu.make_async_remote_copy(
            src_ref=STAGE.at[it],
            dst_ref=GAT.at[it, 1, sender],
            send_sem=cross_send.at[it, side],
            recv_sem=cross_recv.at[it, sender],
            device_id=target,
            device_id_type=MESH,
        )

    under = (jnp.maximum(grp - 1, 0), members - 1)
    over = (jnp.minimum(grp + 1, groups - 1), 0)

    def gather_rows(it):
        def send(o, unused):
            peer_copy(it, o, STAGE.at[it]).start()
            return unused

        lax.fori_loop(1, members, send, 0)

        @pl.when(grp > 0)
        def _():
            cross_copy(it, 0, me, under).start()

        @pl.when(grp < groups - 1)
        def _():
            cross_copy(it, 1, me, over).start()

        GAT[it, 0, me] = STAGE[it]

        def arrive(o, unused):
            peer_copy(it, o, STAGE.at[it]).wait_send()
            peer_arrival(it, lax.rem(me + o, members)).wait_recv()
            return unused

        lax.fori_loop(1, members, arrive, 0)

        @pl.when(grp > 0)
        def _():
            cross_copy(it, 0, me, under).wait_send()

        @pl.when(grp < groups - 1)
        def _():
            cross_copy(it, 1, me, over).wait_send()

        @pl.when(((me == members - 1) & (grp < groups - 1)) | ((me == 0) & (grp > 0)))
        def _():
            def arrive_cross(sender, unused):
                cross_copy(it, 0, sender, under).wait_recv()
                return unused

            lax.fori_loop(0, members, arrive_cross, 0)

    for it in range(2):
        if it == 1:
            start_field(1)
        wait_field(it, 0)

        for k in range(3):
            ACC[k] = jnp.zeros((height, breadth), jnp.float32)

        def first_of(k, n, it=it):
            return W[n + HALO] * R[it, k, n + HALO]

        def add_defect(k, n, value, it=it):
            ACC[k] = ACC[k] + (R[it, k, n + HALO] - value)

        apply_stiffness(first_of, add_defect, 0, layers - 1)
        for k in range(3):
            STAGE[it, k : k + 1] = block_row(ACC[k])
        gather_rows(it)
        correction = coarse_solve(it)
        member_at = lax.broadcasted_iota(jnp.int32, (members, lanes), 0)
        for k in range(3):
            own, other = correction[k][0], correction[k][1]

            def row_of(field, index):
                return jnp.sum(jnp.where(member_at == index, field, 0.0), axis=0, keepdims=True)

            under_row = jnp.where(me == 0, row_of(other, members - 1), row_of(own, me - 1))
            over_row = jnp.where(me == members - 1, row_of(other, 0), row_of(own, me + 1))
            PRO[0, k] = block_plane(under_row)
            PRO[1, k] = block_plane(row_of(own, me))
            PRO[2, k] = block_plane(over_row)

        wait_field(it, 1)

        def second_of(k, n, it=it):
            block = jnp.where(n < 0, 0, jnp.where(n >= layers, 2, 1))
            return first_of(k, n, it) + free_at(n) * PRO[block, k]

        def smooth(k, n, value, it=it):
            S[it, k, n + HALO] = second_of(k, n, it) + W[n + HALO] * (
                R[it, k, n + HALO] - value
            )

        apply_stiffness(second_of, smooth, -1, layers)

        def smoothed_of(k, n, it=it):
            return S[it, k, n + HALO]

        def keep_image(k, n, value, it=it):
            R[it + 1, k, n + HALO] = value

        apply_stiffness(smoothed_of, keep_image, 0, layers - 1)

    ACC[...] = jnp.zeros(ACC.shape, jnp.float32)

    def products(n, unused):
        i = n + HALO
        for k in range(3):
            r, q, t = R[0, k, i], R[1, k, i], R[2, k, i]
            p, s = S[0, k, i], S[1, k, i]
            for index, value in enumerate((r * p, p * q, r * s, q * s, p * t, s * t)):
                ACC[index] = ACC[index] + value
        return unused

    lax.fori_loop(0, layers, products, 0)
    DSUM[...] = jnp.zeros(DSUM.shape, jnp.float32)
    for index in range(6):
        DSUM[0, index : index + 1] = jnp.sum(ACC[index], axis=0, keepdims=True)

    def dot_copy(o):
        return pltpu.make_async_remote_copy(
            src_ref=DSUM.at[0],
            dst_ref=DOT.at[me],
            send_sem=dot_send.at[o],
            recv_sem=dot_recv.at[me],
            device_id=(grp, lax.rem(me + o, members)),
            device_id_type=MESH,
        )

    def dot_arrival(sender):
        return pltpu.make_async_remote_copy(
            src_ref=DSUM.at[0],
            dst_ref=DOT.at[sender],
            send_sem=dot_send.at[0],
            recv_sem=dot_recv.at[sender],
            device_id=(grp, sender),
            device_id_type=MESH,
        )

    def dotg_copy(o):
        return pltpu.make_async_remote_copy(
            src_ref=DSUM.at[1],
            dst_ref=DOTG.at[grp],
            send_sem=dotg_send.at[o],
            recv_sem=dotg_recv.at[grp],
            device_id=(lax.rem(grp + o, groups), me),
            device_id_type=MESH,
        )

    def dotg_arrival(sender):
        return pltpu.make_async_remote_copy(
            src_ref=DSUM.at[1],
            dst_ref=DOTG.at[sender],
            send_sem=dotg_send.at[0],
            recv_sem=dotg_recv.at[sender],
            device_id=(sender, me),
            device_id_type=MESH,
        )

    def exchange(copy, arrival, own, size):
        def send(o, unused):
            copy(o).start()
            return unused

        def arrive(o, unused):
            copy(o).wait_send()
            arrival(lax.rem(own + o, size)).wait_recv()
            return unused

        lax.fori_loop(1, size, send, 0)
        return lambda: lax.fori_loop(1, size, arrive, 0)

    finish = exchange(dot_copy, dot_arrival, me, members)
    DOT[me] = DSUM[0]
    finish()
    DSUM[1] = jnp.sum(DOT[...], axis=0)
    finish = exchange(dotg_copy, dotg_arrival, grp, groups)
    DOTG[grp] = DSUM[1]
    finish()
    sums = jnp.sum(jnp.sum(DOTG[...], axis=0), axis=1, keepdims=True)
    rp, pq, rs, qs, pt, st = [sums[index : index + 1] for index in range(6)]
    alpha = rp / pq
    following = rp - alpha * (rs + pq) + alpha * alpha * qs
    curve = pq - alpha * (pt + qs) + alpha * alpha * st
    beta = following / rp
    alpha_two = following / (curve - beta * following / alpha)
    weight_a = alpha + alpha_two * (1.0 + beta)
    weight_b = alpha * alpha_two

    def finish_layer(n, unused):
        i = n + HALO
        for k in range(3):
            out_u[k, n] = weight_a * S[0, k, i] - weight_b * S[1, k, i]
            out_r[k, n] = R[0, k, i] - weight_a * R[1, k, i] + weight_b * R[2, k, i]
        return unused

    lax.fori_loop(0, layers, finish_layer, 0)


def body(groups, members, load, phases, clamp, phase_moduli):
    _, layers, height, breadth = load.shape
    assert layers == COARSEN
    plane = (height, breadth)
    deep = layers + 2 * HALO
    lanes = (height // COARSEN) * (breadth // COARSEN)
    vmem = pl.BlockSpec(memory_space=pltpu.VMEM)
    dma = pltpu.SemaphoreType.DMA
    f32 = jnp.float32
    return tuple(
        pl.pallas_call(
            functools.partial(kernel, groups, members),
            out_shape=(
                jax.ShapeDtypeStruct(load.shape, f32),
                jax.ShapeDtypeStruct(load.shape, f32),
            ),
            in_specs=[vmem, vmem, vmem, pl.BlockSpec(memory_space=pltpu.SMEM)],
            out_specs=(vmem, vmem),
            scratch_shapes=[
                pltpu.VMEM((3, 3, deep) + plane, f32),
                pltpu.VMEM((2, 3, deep) + plane, f32),
                pltpu.VMEM((deep,) + plane, f32),
                pltpu.VMEM((deep + 1,) + plane, f32),
                pltpu.VMEM((5,) + plane, jnp.int32),
                pltpu.VMEM((2,) + plane, f32),
                pltpu.VMEM((3, 3) + plane, f32),
                pltpu.VMEM((2, 12) + plane, f32),
                pltpu.VMEM((12,) + plane, f32),
                pltpu.VMEM((12,) + plane, f32),
                pltpu.VMEM((6,) + plane, f32),
                pltpu.VMEM((2, 8, lanes), f32),
                pltpu.VMEM((2, 2, members, 8, lanes), f32),
                pltpu.VMEM((members, 8, breadth), f32),
                pltpu.VMEM((2, 8, breadth), f32),
                pltpu.VMEM((groups, 8, breadth), f32),
                dma((10,)),
                dma((10,)),
                dma((2, members)),
                dma((2, members)),
                dma((2, 2)),
                dma((2, members)),
                dma((members,)),
                dma((members,)),
                dma((groups,)),
                dma((groups,)),
            ],
            compiler_params=pltpu.CompilerParams(
                collective_id=0, has_side_effects=True, vmem_limit_bytes=48 * 1024 * 1024
            ),
        )(load, phases, clamp, phase_moduli)
    )


def solution(mesh):
    groups, members = mesh.shape["grp"], mesh.shape["gz"]
    placed = (P(None, ("grp", "gz"), None, None), P(("grp", "gz"), None, None), P(), P())
    return jax.shard_map(
        functools.partial(body, groups, members),
        mesh=mesh,
        in_specs=placed,
        out_specs=(P(None, ("grp", "gz"), None, None), P(None, ("grp", "gz"), None, None)),
        check_vma=False,
    )
```

time: 792 us -> 67.5 us (0.09); the launches traced: 782 us -> 67.3 us
  other arithmetic: 226 us -> 0 us
  local copies, waits for them, and re-layouts: 217 us -> 5.25 us
  blocking collectives: 171 us -> 0 us
  matrix products: 89.6 us -> 0 us
  Pallas kernels: 0 us -> 61.4 us
  starting transfers between devices: 38.5 us -> 0 us
  loops' own time: 20.7 us -> 0 us
  waiting for transfers between devices: 10.6 us -> 0 us
    psum x4 -> x0, blocking collectives: 139 us -> none  [the longest x2 92.8 us: paired_sums(): lax.psum((jnp.sum(residual * preconditioned), jnp.sum(preconditioned * im...]
    slice x280 -> x0, local copies, waits for them, and re-layouts: 102 us -> none  [the longest x144 72.7 us: add_block(): jnp.roll(forces[corner], (offset[1], offset[2]), (2, 3))]
    dot_general x24 -> x0, matrix products: 89.6 us -> none  [add_block(): jnp.einsum('ij,jzyx->izyx', matrix, gathered, precision=lax.Precision.HIG...]
    pallas_call x0 -> x1, Pallas kernels: none -> 61.4 us  [body(): pl.pallas_call(functools.partial(kernel, groups, members), out_shape=(jax...]
    scatter-add x150 -> x0, other arithmetic: 60.7 us -> none  [the longest x144 55.2 us: add_block(): update.at[:, offset[0]:offset[0] + width]]
    while x120 -> x0, other arithmetic: 55.6 us -> none
    ppermute x13 -> x0, starting transfers between devices: 38.5 us -> none  [passed_along(): return lax.ppermute(value, axis, pairs)]
    while x216 -> x0, local copies, waits for them, and re-layouts: 37.6 us -> none
  transfers between devices with their start and end apart: 13 -> 0, of which waited for: 6 -> 0; matrix products, arithmetic and copies ran while one was open for 2% -> 0% of each run, Pallas kernels for 0% -> 0%
where the time goes in v1:
time: 67.5 us; the launch traced here: 67.3 us
  Pallas kernels  61.4 us (91%)
  local copies, waits for them, and re-layouts  5.25 us (8%)
    pallas_call x1, Pallas kernels, body(): pl.pallas_call(functools.partial(kernel, groups, members), out_shape=(jax...  61.4 us
    unnamed x10, local copies, waits for them, and re-layouts  5.25 us

profile of v1, /device:TPU:0, one launch (start us, length us, event | category | flops | bytes accessed | tf_op | source)
XLA Modules:
  0.0 67.3 jit_solution(13615990614534798192)
XLA Ops:
  0.6 0.0 copy-start
  0.6 1.1 %copy-done = f32[3,8,64,128]{3,2,1,0:T(8,128)S(1)} copy-done((f32[3,8,64,128]{3,2,1,0:T(8,128)S(1)}, f32[3,8,64,128]{3,2,1,0:T(8,128)}, u32[]{:S(2)}) %copy-start) | copy-done | bytes 786456
  1.8 0.0 copy-start.1
  1.8 0.9 %copy-done.1 = s32[8,64,128]{2,1,0:T(8,128)S(1)} copy-done((s32[8,64,128]{2,1,0:T(8,128)S(1)}, s32[8,64,128]{2,1,0:T(8,128)}, u32[]{:S(2)}) %copy-start.1) | copy-done | bytes 262168
  2.7 0.0 copy-start.2
  2.7 0.8 %copy-done.2 = s32[64,128]{1,0:T(8,128)S(1)} copy-done((s32[64,128]{1,0:T(8,128)S(1)}, s32[64,128]{1,0:T(8,128)}, u32[]{:S(2)}) %copy-start.2) | copy-done | bytes 32792
  3.5 0.0 copy-start.3
  3.5 0.7 copy-done.3
  4.1 61.4 %shard_map.59 = (f32[3,8,64,128]{3,2,1,0:T(8,128)S(1)}, f32[3,8,64,128]{3,2,1,0:T(8,128)S(1)}) custom-call(f32[3,8,64,128]{3,2,1,0:T(8,128)S(1)} %copy-done, s32[8,64,128]{2,1,0:T(8,128)S(1)} %copy-done.1, s32[64,128]{1,0:T(8,128)S(1)} %copy-done.2, f32[4]{0:T(128)S(1)} %copy-done.3), custom_call_target="tpu_custom_call" | custom-call | tf_op jit(solution)/shard_map/pallas_call | solution.py:750
  65.5 0.9 %copy.8 = f32[3,8,64,128]{3,2,1,0:T(8,128)} copy(f32[3,8,64,128]{3,2,1,0:T(8,128)S(1)} %get-tuple-element.4) | data formatting | bytes 1572864
  66.4 0.9 %copy.9 = f32[3,8,64,128]{3,2,1,0:T(8,128)} copy(f32[3,8,64,128]{3,2,1,0:T(8,128)S(1)} %get-tuple-element.5) | data formatting | bytes 1572864
Async XLA Ops:
  0.6 1.1 %copy-start = (f32[3,8,64,128]{3,2,1,0:T(8,128)S(1)}, f32[3,8,64,128]{3,2,1,0:T(8,128)}, u32[]{:S(2)}) copy-start(f32[3,8,64,128]{3,2,1,0:T(8,128)} %load.1) | copy-start | bytes 2359300
  1.8 0.9 %copy-start.1 = (s32[8,64,128]{2,1,0:T(8,128)S(1)}, s32[8,64,128]{2,1,0:T(8,128)}, u32[]{:S(2)}) copy-start(s32[8,64,128]{2,1,0:T(8,128)} %phases.1) | copy-start | bytes 786436
  2.7 0.8 %copy-start.2 = (s32[64,128]{1,0:T(8,128)S(1)}, s32[64,128]{1,0:T(8,128)}, u32[]{:S(2)}) copy-start(s32[64,128]{1,0:T(8,128)} %clamp.1) | copy-start | bytes 98308
  3.5 0.7 copy-start.3

commit v2 on v1

--- a/solution.py
+++ b/solution.py
@@ -146,21 +146,23 @@
     out_u,
     out_r,
     R,
+    LABEL,
+    HELD,
+    PART,
+    SEAM,
     S,
     W,
     MOD,
     PH,
     FREE,
     PRO,
-    FWD,
-    FSUM,
-    CARRY,
     ACC,
     STAGE,
     GAT,
     DOT,
     DSUM,
     DOTG,
+    in_sem,
     halo_send,
     halo_recv,
     gat_send,
@@ -201,35 +203,13 @@
 
     lax.fori_loop(1, tiles, greet, 0)
 
-    rows_at = lax.broadcasted_iota(jnp.int32, (height, breadth), 0)
-    columns_at = lax.broadcasted_iota(jnp.int32, (height, breadth), 1)
-    inside = (rows_at < height - 1) & (columns_at < breadth - 1)
-
-    def moduli_of(labels, depth):
-        picked = jnp.zeros((height, breadth), jnp.float32)
-        for phase in range(PHASES):
-            picked = jnp.where(labels == phase, phase_moduli[phase], picked)
-        keep = jnp.where((depth >= 0) & (depth < tiles * layers - 1), 1.0, 0.0)
-        return jnp.where(inside, picked, 0.0) * keep
-
-    first_depth = tile * layers
-    bottom = jnp.where(tile == 0, 1.0, 0.0)
-    held = jnp.where(clamp[...] == 1, 1.0, 0.0) * bottom
-    FREE[0] = 1.0 - held
-    FREE[1] = jnp.ones((height, breadth), jnp.float32)
-
-    ACC[0] = jnp.zeros((height, breadth), jnp.float32)
-
-    def own_layer(n, unused):
-        mod = moduli_of(phases[n], first_depth + n)
-        MOD[n + 3] = mod
-        ACC[0] = ACC[0] + mod
-        free = FREE[jnp.where(n == 0, 0, 1)]
-        for k in range(3):
-            R[0, k, n + HALO] = free * load[k, n]
-        return unused
-
-    lax.fori_loop(0, layers, own_layer, 0)
+    incoming = [
+        pltpu.make_async_copy(load, R.at[0, :, HALO : HALO + layers], in_sem.at[0]),
+        pltpu.make_async_copy(phases, LABEL, in_sem.at[1]),
+        pltpu.make_async_copy(clamp, HELD, in_sem.at[2]),
+    ]
+    for copy in incoming:
+        copy.start()
 
     @pl.when(tile == 0)
     def _():
@@ -244,6 +224,14 @@
             R[it, :, layers + HALO :] = jnp.zeros((3, HALO, height, breadth), jnp.float32)
 
     STAGE[...] = jnp.zeros(STAGE.shape, jnp.float32)
+    for copy in incoming:
+        copy.wait()
+    first_depth = tile * layers
+    bottom = jnp.where(tile == 0, 1.0, 0.0)
+    free_plane = 1.0 - jnp.where(HELD[...] == 1, 1.0, 0.0) * bottom
+    FREE[...] = free_plane
+    for k in range(3):
+        R[0, k, HALO] = free_plane * R[0, k, HALO]
 
     pl.semaphore_wait(barrier, tiles - 1)
 
@@ -284,8 +272,8 @@
             R.at[it, :, HALO + depth], R.at[it, :, HALO + layers + depth], 4 + it * 4 + depth
         )
 
-    phases_up = to_above(phases.at[layers - 3 : layers], PH.at[0:3], 0)
-    phases_down = to_below(phases.at[0:2], PH.at[3:5], 1)
+    phases_up = to_above(LABEL.at[layers - 3 : layers], PH.at[0:3], 0)
+    phases_down = to_below(LABEL.at[0:2], PH.at[3:5], 1)
 
     def start_field(it):
         for depth in range(HALO):
@@ -318,6 +306,27 @@
         phases_down.start()
 
     start_field(0)
+
+    rows_at = lax.broadcasted_iota(jnp.int32, (height, breadth), 0)
+    columns_at = lax.broadcasted_iota(jnp.int32, (height, breadth), 1)
+    inside = (rows_at < height - 1) & (columns_at < breadth - 1)
+
+    def moduli_of(labels, depth):
+        picked = jnp.zeros((height, breadth), jnp.float32)
+        for phase in range(PHASES):
+            picked = jnp.where(labels == phase, phase_moduli[phase], picked)
+        keep = jnp.where((depth >= 0) & (depth < tiles * layers - 1), 1.0, 0.0)
+        return jnp.where(inside, picked, 0.0) * keep
+
+    ACC[0] = jnp.zeros((height, breadth), jnp.float32)
+
+    def own_layer(n, unused):
+        mod = moduli_of(LABEL[n], first_depth + n)
+        MOD[n + 3] = mod
+        ACC[0] = ACC[0] + mod
+        return unused
+
+    lax.fori_loop(0, layers, own_layer, 0)
 
     lanes = coarse_height * coarse_breadth
     fine_at = lax.broadcasted_iota(jnp.int32, (breadth, lanes), 0)
@@ -363,21 +372,6 @@
     for it in range(2):
         STAGE[it, 3:4] = coarse_row
 
-    @pl.when(has_above)
-    def _():
-        phases_up.wait_send()
-        phases_down.wait_recv()
-
-    @pl.when(has_below)
-    def _():
-        phases_down.wait_send()
-        phases_up.wait_recv()
-
-    for n in range(3):
-        MOD[n] = moduli_of(PH[n], first_depth - 3 + n)
-    for n in range(2):
-        MOD[layers + 3 + n] = moduli_of(PH[3 + n], first_depth + layers + n)
-
     def back_x(value):
         return pltpu.roll(value, 1, 1)
 
@@ -387,74 +381,117 @@
     def fore_x(value):
         return pltpu.roll(value, breadth - 1, 1)
 
-    def fore_y(value):
-        return pltpu.roll(value, height - 1, 0)
-
-    def free_at(n):
-        return FREE[jnp.where(n == 0, 0, 1)]
-
-    def inverse_layer(i, unused):
-        pair = MOD[i] + MOD[i + 1]
+    def inverse_layer(n, free):
+        pair = MOD[n + 2] + MOD[n + 3]
         pair = pair + back_x(pair)
         pair = pair + back_y(pair)
-        free = free_at(i - HALO)
-        depth = first_depth + i - HALO
+        depth = first_depth + n
         valid = (depth >= 0) & (depth < tiles * layers)
-        diagonal = jnp.where(valid, free * (entry * pair) + 1.0 - free, 1.0)
-        W[i] = omega / diagonal
+        diagonal = entry * pair
+        if free is not None:
+            diagonal = free * diagonal + 1.0 - free
+        W[n + HALO] = omega / jnp.where(valid, diagonal, 1.0)
+
+    def inverse_inner(n, unused):
+        inverse_layer(n, None)
         return unused
 
-    lax.fori_loop(0, layers + 2 * HALO, inverse_layer, 0)
-
-    def modes_into(get, n):
-        slot = lax.rem(n + 4, 2)
-        free = free_at(n)
-        for k in range(3):
-            modes = plane_modes(free * get(k, n), fore_y, fore_x)
-            for b in (0, 1):
-                for c in (0, 1):
-                    FWD[slot, 4 * k + 2 * b + c] = modes[b][c]
-
-    def apply_stiffness(get, put, lowest, highest):
-        modes_into(get, jnp.int32(lowest - 1))
-        CARRY[...] = jnp.zeros(CARRY.shape, jnp.float32)
-
-        def layer(v, unused):
-            modes_into(get, v + 1)
-            lower = lax.rem(v + 4, 2)
-            upper = lax.rem(v + 5, 2)
-
-            def chunk(j, nothing):
-                rows = pl.ds(pl.multiple_of(j * 8, 8), 8)
-
-                def of(slot):
-                    return [
-                        [[FWD[slot, 4 * k + 2 * b + c, rows] for c in (0, 1)] for b in (0, 1)]
+    lax.fori_loop(1, layers, inverse_inner, 0)
+
+    def halo_moduli():
+        @pl.when(has_above)
+        def _():
+            phases_up.wait_send()
+            phases_down.wait_recv()
+
+        @pl.when(has_below)
+        def _():
+            phases_down.wait_send()
+            phases_up.wait_recv()
+
+        for n in range(3):
+            MOD[n] = moduli_of(PH[n], first_depth - 3 + n)
+        for n in range(2):
+            MOD[layers + 3 + n] = moduli_of(PH[3 + n], first_depth + layers + n)
+        for n in (-2, -1, 0, layers, layers + 1):
+            inverse_layer(n, FREE[...] if n == 0 else None)
+
+    chunks = height // 8
+    row_at = lax.broadcasted_iota(jnp.int32, (8, breadth), 0)
+    first_row = row_at == 0
+
+    def sweep(get, put, start, stop, put_first=None, put_last=None):
+        for n in range(start, stop + 1):
+            for k in range(3):
+                SEAM[n + HALO, k] = jnp.zeros((8, breadth), jnp.float32)
+
+        def chunk(j, unused):
+            rows = pl.ds(pl.multiple_of(j * 8, 8), 8)
+            following_rows = pl.ds(pl.multiple_of(lax.rem(j + 1, chunks) * 8, 8), 8)
+
+            def modes(n, masked):
+                out = []
+                for k in range(3):
+                    here, after = get(k, n, rows), get(k, n, following_rows)
+                    if masked:
+                        here, after = FREE[rows] * here, FREE[following_rows] * after
+                    over = pltpu.roll(jnp.where(first_row, after, here), 7, 0)
+                    here_x, over_x = fore_x(here), fore_x(over)
+                    sums = here + here_x, over + over_x
+                    steps = here_x - here, over_x - over
+                    out.append(
+                        [
+                            [sums[0] + sums[1], steps[0] + steps[1]],
+                            [sums[1] - sums[0], steps[1] - steps[0]],
+                        ]
+                    )
+                return out
+
+            def emit(n, force, masked, to):
+                for k in range(3):
+                    e = [
+                        (force[k][b][0] - force[k][b][1])
+                        + back_x(force[k][b][0] + force[k][b][1])
+                        for b in (0, 1)
+                    ]
+                    turned = pltpu.roll(e[0] + e[1], 1, 0)
+                    total = (e[0] - e[1]) + jnp.where(first_row, SEAM[n + HALO, k], turned)
+                    SEAM[n + HALO, k] = turned
+                    if masked:
+                        free = FREE[rows]
+                        total = free * total + (1.0 - free) * get(k, n, rows)
+                    to(k, n, rows, total)
+
+            def step(v, below, carry, static):
+                above = modes(v + 1, static and v + 1 == 0)
+                low, high = voxel_forces(below, above, MOD[v + 3, rows], 1.0)
+                if carry is None:
+                    if put_first is not None:
+                        emit(v, low, static and v == 0, put_first)
+                else:
+                    force = [
+                        [[carry[k][b][c] + low[k][b][c] for c in (0, 1)] for b in (0, 1)]
                         for k in range(3)
                     ]
-
-                low, high = voxel_forces(of(lower), of(upper), MOD[v + 3, rows], 1.0)
-                for k in range(3):
-                    for b in (0, 1):
-                        for c in (0, 1):
-                            index = 4 * k + 2 * b + c
-                            FSUM[index, rows] = CARRY[index, rows] + low[k][b][c]
-                            CARRY[index, rows] = high[k][b][c]
-                return nothing
-
-            lax.fori_loop(0, height // 8, chunk, 0, unroll=True)
-
-            @pl.when(v >= lowest)
-            def _():
-                free = free_at(v)
-                for k in range(3):
-                    force = [[FSUM[4 * k + 2 * b + c] for c in (0, 1)] for b in (0, 1)]
-                    total = plane_forces(force, back_y, back_x)
-                    put(k, v, free * total + (1.0 - free) * get(k, v))
-
+                    emit(v, force, static and v == 0, put)
+                return above, high
+
+            below, carry = modes(start, start == 0), None
+            v = start
+            while v < stop and (v <= max(start, 0)):
+                below, carry = step(v, below, carry, True)
+                v += 1
+            if v < stop:
+
+                def inner(at, state):
+                    return step(at, state[0], state[1], False)
+
+                below, carry = lax.fori_loop(v, stop, inner, (below, carry), unroll=True)
+            if put_last is not None:
+                emit(stop, carry, stop == 0, put_last)
             return unused
 
-        lax.fori_loop(lowest - 1, highest + 1, layer, 0)
+        lax.fori_loop(0, chunks, chunk, 0)
 
     def coarse_ahead(value, by):
         return pltpu.roll(value, lanes - by, 2)
@@ -591,18 +628,34 @@
     for it in range(2):
         if it == 1:
             start_field(1)
-        wait_field(it, 0)
 
         for k in range(3):
             ACC[k] = jnp.zeros((height, breadth), jnp.float32)
 
-        def first_of(k, n, it=it):
-            return W[n + HALO] * R[it, k, n + HALO]
-
-        def add_defect(k, n, value, it=it):
-            ACC[k] = ACC[k] + (R[it, k, n + HALO] - value)
-
-        apply_stiffness(first_of, add_defect, 0, layers - 1)
+        def first_of(k, n, rows, it=it):
+            return W[n + HALO, rows] * R[it, k, n + HALO, rows]
+
+        def add_defect(k, n, rows, value, it=it):
+            ACC[k, rows] = ACC[k, rows] + (R[it, k, n + HALO, rows] - value)
+
+        def part(index):
+            def to(k, n, rows, value):
+                PART[index, k, rows] = value
+
+            return to
+
+        def with_part(index):
+            def to(k, n, rows, value):
+                add_defect(k, n, rows, PART[index, k, rows] + value)
+
+            return to
+
+        sweep(first_of, add_defect, 1, layers - 1, part(0), part(1))
+        if it == 0:
+            halo_moduli()
+        wait_field(it, 0)
+        sweep(first_of, add_defect, -1, 1, None, with_part(0))
+        sweep(first_of, add_defect, layers - 1, layers, with_part(1), None)
         for k in range(3):
             STAGE[it, k : k + 1] = block_row(ACC[k])
         gather_rows(it)
@@ -622,24 +675,27 @@
 
         wait_field(it, 1)
 
-        def second_of(k, n, it=it):
+        def second_of(k, n, rows, it=it):
             block = jnp.where(n < 0, 0, jnp.where(n >= layers, 2, 1))
-            return first_of(k, n, it) + free_at(n) * PRO[block, k]
-
-        def smooth(k, n, value, it=it):
-            S[it, k, n + HALO] = second_of(k, n, it) + W[n + HALO] * (
-                R[it, k, n + HALO] - value
+            spread = PRO[block, k, rows]
+            if isinstance(n, int) and n == 0:
+                spread = FREE[rows] * spread
+            return first_of(k, n, rows, it) + spread
+
+        def smooth(k, n, rows, value, it=it):
+            S[it, k, n + HALO, rows] = second_of(k, n, rows, it) + W[n + HALO, rows] * (
+                R[it, k, n + HALO, rows] - value
             )
 
-        apply_stiffness(second_of, smooth, -1, layers)
-
-        def smoothed_of(k, n, it=it):
-            return S[it, k, n + HALO]
-
-        def keep_image(k, n, value, it=it):
-            R[it + 1, k, n + HALO] = value
-
-        apply_stiffness(smoothed_of, keep_image, 0, layers - 1)
+        sweep(second_of, smooth, -2, layers + 1)
+
+        def smoothed_of(k, n, rows, it=it):
+            return S[it, k, n + HALO, rows]
+
+        def keep_image(k, n, rows, value, it=it):
+            R[it + 1, k, n + HALO, rows] = value
+
+        sweep(smoothed_of, keep_image, -1, layers)
 
     ACC[...] = jnp.zeros(ACC.shape, jnp.float32)
 
@@ -744,6 +800,7 @@
     deep = layers + 2 * HALO
     lanes = (height // COARSEN) * (breadth // COARSEN)
     vmem = pl.BlockSpec(memory_space=pltpu.VMEM)
+    hbm = pl.BlockSpec(memory_space=pltpu.HBM)
     dma = pltpu.SemaphoreType.DMA
     f32 = jnp.float32
     return tuple(
@@ -753,25 +810,27 @@
                 jax.ShapeDtypeStruct(load.shape, f32),
                 jax.ShapeDtypeStruct(load.shape, f32),
             ),
-            in_specs=[vmem, vmem, vmem, pl.BlockSpec(memory_space=pltpu.SMEM)],
+            in_specs=[hbm, hbm, hbm, pl.BlockSpec(memory_space=pltpu.SMEM)],
             out_specs=(vmem, vmem),
             scratch_shapes=[
                 pltpu.VMEM((3, 3, deep) + plane, f32),
+                pltpu.VMEM((layers,) + plane, jnp.int32),
+                pltpu.VMEM(plane, jnp.int32),
+                pltpu.VMEM((2, 3) + plane, f32),
+                pltpu.VMEM((deep, 3, 8, breadth), f32),
                 pltpu.VMEM((2, 3, deep) + plane, f32),
                 pltpu.VMEM((deep,) + plane, f32),
                 pltpu.VMEM((deep + 1,) + plane, f32),
                 pltpu.VMEM((5,) + plane, jnp.int32),
-                pltpu.VMEM((2,) + plane, f32),
+                pltpu.VMEM(plane, f32),
                 pltpu.VMEM((3, 3) + plane, f32),
-                pltpu.VMEM((2, 12) + plane, f32),
-                pltpu.VMEM((12,) + plane, f32),
-                pltpu.VMEM((12,) + plane, f32),
                 pltpu.VMEM((6,) + plane, f32),
                 pltpu.VMEM((2, 8, lanes), f32),
                 pltpu.VMEM((2, 2, members, 8, lanes), f32),
                 pltpu.VMEM((members, 8, breadth), f32),
                 pltpu.VMEM((2, 8, breadth), f32),
                 pltpu.VMEM((groups, 8, breadth), f32),
+                dma((3,)),
                 dma((10,)),
                 dma((10,)),
                 dma((2, members)),

time: 67.5 us -> 61 us (0.904)
  Pallas kernels: 61.4 us -> 54.8 us
    pallas_call x1, Pallas kernels: 61.4 us -> 54.8 us  [body(): pl.pallas_call(functools.partial(kernel, groups, members), out_shape=(jax...]
where the time goes in v2:
time: 61 us; the launch traced here: 60.7 us
  Pallas kernels  54.8 us (90%)
  local copies, waits for them, and re-layouts  5.25 us (9%)
  between operations  0.65 us (1%)
    pallas_call x1, Pallas kernels, body(): pl.pallas_call(functools.partial(kernel, groups, members), out_shape=(jax...  54.8 us
    unnamed x10, local copies, waits for them, and re-layouts  5.25 us

profile of v2, /device:TPU:0, one launch (start us, length us, event | category | flops | bytes accessed | tf_op | source)
XLA Modules:
  0.0 60.7 jit_solution(6796576788716158125)
XLA Ops:
  0.6 0.0 copy-start
  0.6 1.1 %copy-done = f32[3,8,64,128]{3,2,1,0:T(8,128)S(1)} copy-done((f32[3,8,64,128]{3,2,1,0:T(8,128)S(1)}, f32[3,8,64,128]{3,2,1,0:T(8,128)}, u32[]{:S(2)}) %copy-start) | copy-done | bytes 786456
  1.8 0.0 copy-start.1
  1.8 0.9 %copy-done.1 = s32[8,64,128]{2,1,0:T(8,128)S(1)} copy-done((s32[8,64,128]{2,1,0:T(8,128)S(1)}, s32[8,64,128]{2,1,0:T(8,128)}, u32[]{:S(2)}) %copy-start.1) | copy-done | bytes 262168
  2.7 0.0 copy-start.2
  2.7 0.8 %copy-done.2 = s32[64,128]{1,0:T(8,128)S(1)} copy-done((s32[64,128]{1,0:T(8,128)S(1)}, s32[64,128]{1,0:T(8,128)}, u32[]{:S(2)}) %copy-start.2) | copy-done | bytes 32792
  3.5 0.0 copy-start.3
  3.5 0.7 %copy-done.3 = f32[4]{0:T(128)S(1)} copy-done((f32[4]{0:T(128)S(1)}, f32[4]{0:T(128)}, u32[]{:S(2)}) %copy-start.3) | copy-done | bytes 40
  4.1 54.8 %shard_map.59 = (f32[3,8,64,128]{3,2,1,0:T(8,128)S(1)}, f32[3,8,64,128]{3,2,1,0:T(8,128)S(1)}) custom-call(f32[3,8,64,128]{3,2,1,0:T(8,128)S(1)} %copy-done, s32[8,64,128]{2,1,0:T(8,128)S(1)} %copy-done.1, s32[64,128]{1,0:T(8,128)S(1)} %copy-done.2, f32[4]{0:T(128)S(1)} %copy-done.3), custom_call_target="tpu_custom_call" | custom-call | tf_op jit(solution)/shard_map/pallas_call | solution.py:807
  59.0 0.9 %copy.8 = f32[3,8,64,128]{3,2,1,0:T(8,128)} copy(f32[3,8,64,128]{3,2,1,0:T(8,128)S(1)} %get-tuple-element.4) | data formatting | bytes 1572864
  59.9 0.9 %copy.9 = f32[3,8,64,128]{3,2,1,0:T(8,128)} copy(f32[3,8,64,128]{3,2,1,0:T(8,128)S(1)} %get-tuple-element.5) | data formatting | bytes 1572864
Async XLA Ops:
  0.6 1.1 %copy-start = (f32[3,8,64,128]{3,2,1,0:T(8,128)S(1)}, f32[3,8,64,128]{3,2,1,0:T(8,128)}, u32[]{:S(2)}) copy-start(f32[3,8,64,128]{3,2,1,0:T(8,128)} %load.1) | copy-start | bytes 2359300
  1.8 0.9 %copy-start.1 = (s32[8,64,128]{2,1,0:T(8,128)S(1)}, s32[8,64,128]{2,1,0:T(8,128)}, u32[]{:S(2)}) copy-start(s32[8,64,128]{2,1,0:T(8,128)} %phases.1) | copy-start | bytes 786436
  2.7 0.8 %copy-start.2 = (s32[64,128]{1,0:T(8,128)S(1)}, s32[64,128]{1,0:T(8,128)}, u32[]{:S(2)}) copy-start(s32[64,128]{1,0:T(8,128)} %clamp.1) | copy-start | bytes 98308
  3.5 0.7 %copy-start.3 = (f32[4]{0:T(128)S(1)}, f32[4]{0:T(128)}, u32[]{:S(2)}) copy-start(f32[4]{0:T(128)} %phase_moduli.1) | copy-start | bytes 52

commit v3 on v2

--- a/solution.py
+++ b/solution.py
@@ -191,17 +191,39 @@
     GAT[...] = jnp.zeros(GAT.shape, jnp.float32)
     barrier = pltpu.get_barrier_semaphore()
 
-    def greet(o, unused):
-        other = lax.rem(tile + o, tiles)
-        pl.semaphore_signal(
-            barrier,
-            inc=1,
-            device_id=(other // members, lax.rem(other, members)),
-            device_id_type=MESH,
-        )
+    def greet(to):
+        pl.semaphore_signal(barrier, inc=1, device_id=to, device_id_type=MESH)
+
+    def greet_member(o, unused):
+        greet((grp, lax.rem(me + o, members)))
         return unused
 
-    lax.fori_loop(1, tiles, greet, 0)
+    def greet_group(o, unused):
+        greet((lax.rem(grp + o, groups), me))
+        return unused
+
+    lax.fori_loop(1, members, greet_member, 0)
+    lax.fori_loop(1, groups, greet_group, 0)
+
+    @pl.when((me == 0) & (grp > 0))
+    def _():
+        def greet_under(m, unused):
+            greet((grp - 1, m))
+            return unused
+
+        lax.fori_loop(0, members, greet_under, 0)
+
+    @pl.when((me == members - 1) & (grp < groups - 1))
+    def _():
+        def greet_over(m, unused):
+            greet((grp + 1, m))
+            return unused
+
+        lax.fori_loop(0, members, greet_over, 0)
+
+    greeted = (
+        members - 1 + groups - 1 + jnp.where(grp > 0, 1, 0) + jnp.where(grp < groups - 1, 1, 0)
+    )
 
     incoming = [
         pltpu.make_async_copy(load, R.at[0, :, HALO : HALO + layers], in_sem.at[0]),
@@ -233,7 +255,54 @@
     for k in range(3):
         R[0, k, HALO] = free_plane * R[0, k, HALO]
 
-    pl.semaphore_wait(barrier, tiles - 1)
+    rows_at = lax.broadcasted_iota(jnp.int32, (height, breadth), 0)
+    columns_at = lax.broadcasted_iota(jnp.int32, (height, breadth), 1)
+    inside = (rows_at < height - 1) & (columns_at < breadth - 1)
+
+    def moduli_of(labels, depth):
+        picked = jnp.zeros((height, breadth), jnp.float32)
+        for phase in range(PHASES):
+            picked = jnp.where(labels == phase, phase_moduli[phase], picked)
+        keep = jnp.where((depth >= 0) & (depth < tiles * layers - 1), 1.0, 0.0)
+        return jnp.where(inside, picked, 0.0) * keep
+
+    ACC[0] = jnp.zeros((height, breadth), jnp.float32)
+
+    def own_layer(n, unused):
+        mod = moduli_of(LABEL[n], first_depth + n)
+        MOD[n + 3] = mod
+        ACC[0] = ACC[0] + mod
+        return unused
+
+    lax.fori_loop(0, layers, own_layer, 0)
+
+    def back_x(value):
+        return pltpu.roll(value, 1, 1)
+
+    def back_y(value):
+        return pltpu.roll(value, 1, 0)
+
+    def fore_x(value):
+        return pltpu.roll(value, breadth - 1, 1)
+
+    def inverse_layer(n, free):
+        pair = MOD[n + 2] + MOD[n + 3]
+        pair = pair + back_x(pair)
+        pair = pair + back_y(pair)
+        depth = first_depth + n
+        valid = (depth >= 0) & (depth < tiles * layers)
+        diagonal = entry * pair
+        if free is not None:
+            diagonal = free * diagonal + 1.0 - free
+        W[n + HALO] = omega / jnp.where(valid, diagonal, 1.0)
+
+    def inverse_inner(n, unused):
+        inverse_layer(n, None)
+        return unused
+
+    lax.fori_loop(1, layers, inverse_inner, 0)
+
+    pl.semaphore_wait(barrier, greeted)
 
     above_tile = jnp.minimum(tile + 1, tiles - 1)
     below_tile = jnp.maximum(tile - 1, 0)
@@ -306,27 +375,6 @@
         phases_down.start()
 
     start_field(0)
-
-    rows_at = lax.broadcasted_iota(jnp.int32, (height, breadth), 0)
-    columns_at = lax.broadcasted_iota(jnp.int32, (height, breadth), 1)
-    inside = (rows_at < height - 1) & (columns_at < breadth - 1)
-
-    def moduli_of(labels, depth):
-        picked = jnp.zeros((height, breadth), jnp.float32)
-        for phase in range(PHASES):
-            picked = jnp.where(labels == phase, phase_moduli[phase], picked)
-        keep = jnp.where((depth >= 0) & (depth < tiles * layers - 1), 1.0, 0.0)
-        return jnp.where(inside, picked, 0.0) * keep
-
-    ACC[0] = jnp.zeros((height, breadth), jnp.float32)
-
-    def own_layer(n, unused):
-        mod = moduli_of(LABEL[n], first_depth + n)
-        MOD[n + 3] = mod
-        ACC[0] = ACC[0] + mod
-        return unused
-
-    lax.fori_loop(0, layers, own_layer, 0)
 
     lanes = coarse_height * coarse_breadth
     fine_at = lax.broadcasted_iota(jnp.int32, (breadth, lanes), 0)
@@ -346,21 +394,37 @@
         0.0,
     ).astype(jnp.float32)
 
-    def block_row(plane):
-        summed = jnp.sum(plane.reshape(coarse_height, COARSEN, breadth), axis=1)
+    def block_rows(planes):
+        summed = [
+            jnp.sum(plane.reshape(coarse_height, COARSEN, breadth), axis=1) for plane in planes
+        ]
         wide = jnp.dot(
-            summed, gather_x, precision=lax.Precision.HIGHEST, preferred_element_type=jnp.float32
-        )
-        return jnp.sum(wide * row_mask, axis=0, keepdims=True)
-
-    def block_plane(row):
-        wide = jnp.broadcast_to(row, (coarse_height, lanes)) * row_mask
+            jnp.concatenate(summed, 0),
+            gather_x,
+            precision=lax.Precision.HIGHEST,
+            preferred_element_type=jnp.float32,
+        )
+        return [
+            jnp.sum(
+                wide[i * coarse_height : (i + 1) * coarse_height] * row_mask, axis=0, keepdims=True
+            )
+            for i in range(len(planes))
+        ]
+
+    def block_planes(rows):
+        wide = jnp.concatenate(
+            [jnp.broadcast_to(row, (coarse_height, lanes)) * row_mask for row in rows], 0
+        )
         narrow = jnp.dot(
             wide, spread_x, precision=lax.Precision.HIGHEST, preferred_element_type=jnp.float32
         )
-        return jnp.broadcast_to(
-            narrow[:, None, :], (coarse_height, COARSEN, breadth)
-        ).reshape(height, breadth)
+        return [
+            jnp.broadcast_to(
+                narrow[i * coarse_height : (i + 1) * coarse_height][:, None, :],
+                (coarse_height, COARSEN, breadth),
+            ).reshape(height, breadth)
+            for i in range(len(rows))
+        ]
 
     lane_row = lax.broadcasted_iota(jnp.int32, (1, lanes), 1)
     coarse_keep = (
@@ -368,35 +432,9 @@
         & (lax.rem(lane_row, coarse_breadth) < coarse_breadth - 1)
     )
     in_group = jnp.where(me < members - 1, 1.0 / (COARSEN**3), 0.0)
-    coarse_row = jnp.where(coarse_keep, block_row(ACC[0]), 0.0) * in_group
+    coarse_row = jnp.where(coarse_keep, block_rows([ACC[0]])[0], 0.0) * in_group
     for it in range(2):
         STAGE[it, 3:4] = coarse_row
-
-    def back_x(value):
-        return pltpu.roll(value, 1, 1)
-
-    def back_y(value):
-        return pltpu.roll(value, 1, 0)
-
-    def fore_x(value):
-        return pltpu.roll(value, breadth - 1, 1)
-
-    def inverse_layer(n, free):
-        pair = MOD[n + 2] + MOD[n + 3]
-        pair = pair + back_x(pair)
-        pair = pair + back_y(pair)
-        depth = first_depth + n
-        valid = (depth >= 0) & (depth < tiles * layers)
-        diagonal = entry * pair
-        if free is not None:
-            diagonal = free * diagonal + 1.0 - free
-        W[n + HALO] = omega / jnp.where(valid, diagonal, 1.0)
-
-    def inverse_inner(n, unused):
-        inverse_layer(n, None)
-        return unused
-
-    lax.fori_loop(1, layers, inverse_inner, 0)
 
     def halo_moduli():
         @pl.when(has_above)
@@ -656,22 +694,27 @@
         wait_field(it, 0)
         sweep(first_of, add_defect, -1, 1, None, with_part(0))
         sweep(first_of, add_defect, layers - 1, layers, with_part(1), None)
-        for k in range(3):
-            STAGE[it, k : k + 1] = block_row(ACC[k])
+        for k, row in enumerate(block_rows([ACC[k] for k in range(3)])):
+            STAGE[it, k : k + 1] = row
         gather_rows(it)
         correction = coarse_solve(it)
         member_at = lax.broadcasted_iota(jnp.int32, (members, lanes), 0)
+
+        def row_of(field, index):
+            return jnp.sum(jnp.where(member_at == index, field, 0.0), axis=0, keepdims=True)
+
+        spread_rows = []
         for k in range(3):
             own, other = correction[k][0], correction[k][1]
-
-            def row_of(field, index):
-                return jnp.sum(jnp.where(member_at == index, field, 0.0), axis=0, keepdims=True)
-
-            under_row = jnp.where(me == 0, row_of(other, members - 1), row_of(own, me - 1))
-            over_row = jnp.where(me == members - 1, row_of(other, 0), row_of(own, me + 1))
-            PRO[0, k] = block_plane(under_row)
-            PRO[1, k] = block_plane(row_of(own, me))
-            PRO[2, k] = block_plane(over_row)
+            spread_rows.append(
+                jnp.where(me == 0, row_of(other, members - 1), row_of(own, me - 1))
+            )
+            spread_rows.append(row_of(own, me))
+            spread_rows.append(
+                jnp.where(me == members - 1, row_of(other, 0), row_of(own, me + 1))
+            )
+        for index, plane in enumerate(block_planes(spread_rows)):
+            PRO[index % 3, index // 3] = plane
 
         wait_field(it, 1)
 
@@ -843,7 +886,7 @@
                 dma((groups,)),
             ],
             compiler_params=pltpu.CompilerParams(
-                collective_id=0, has_side_effects=True, vmem_limit_bytes=48 * 1024 * 1024
+                collective_id=0, has_side_effects=True, vmem_limit_bytes=67043328
             ),
         )(load, phases, clamp, phase_moduli)
     )

time: 61 us -> 58.4 us (0.957)
  local copies, waits for them, and re-layouts: 5.25 us -> 3.04 us
    unnamed x10 -> x4, local copies, waits for them, and re-layouts: 5.25 us -> 3.04 us
where the time goes in v3:
time: 58.4 us; the launch traced here: 58.2 us
  Pallas kernels  54.5 us (93%)
  local copies, waits for them, and re-layouts  3.04 us (5%)
  between operations  0.65 us (1%)
    pallas_call x1, Pallas kernels, body(): pl.pallas_call(functools.partial(kernel, groups, members), out_shape=(jax...  54.5 us
    unnamed x4, local copies, waits for them, and re-layouts  3.04 us

profile of v3, /device:TPU:0, one launch (start us, length us, event | category | flops | bytes accessed | tf_op | source)
XLA Modules:
  0.0 58.2 jit_solution(9253219970837132173)
XLA Ops:
  0.6 54.5 %shard_map.59 = (f32[3,8,64,128]{3,2,1,0:T(8,128)}, f32[3,8,64,128]{3,2,1,0:T(8,128)}) custom-call(f32[3,8,64,128]{3,2,1,0:T(8,128)} %load.1, s32[8,64,128]{2,1,0:T(8,128)} %phases.1, s32[64,128]{1,0:T(8,128)} %clamp.1, f32[4]{0:T(128)} %phase_moduli.1), custom_call_target="tpu_custom_call" | custom-call | tf_op jit(solution)/shard_map/pallas_call | solution.py:850
  55.2 0.0 copy-start
  55.2 2.2 %copy.8 = f32[3,8,64,128]{3,2,1,0:T(8,128)} copy(f32[3,8,64,128]{3,2,1,0:T(8,128)} %get-tuple-element.4) | data formatting | bytes 1572864
  57.4 0.0 copy-done
  57.4 0.9 %copy.9 = f32[3,8,64,128]{3,2,1,0:T(8,128)} copy(f32[3,8,64,128]{3,2,1,0:T(8,128)S(1)} %copy-done) | data formatting | bytes 1572864
Async XLA Ops:
  55.2 2.2 %copy-start = (f32[3,8,64,128]{3,2,1,0:T(8,128)S(1)}, f32[3,8,64,128]{3,2,1,0:T(8,128)}, u32[]{:S(2)}) copy-start(f32[3,8,64,128]{3,2,1,0:T(8,128)} %get-tuple-element.5) | copy-start | bytes 2359300
